TPU v7x, 128 devices: a whole 4x4x4 slice. The times are simulated.
128 devices in a mesh: sub: 32 (over x, z, core), help: 4 (over y).
Axes of the slice: x: 4, y: 4, z: 4, core: 2. Of those that a mesh axis runs over, the one named last changes fastest.
Arguments:
- right_side: float32 [32, 1024, 256], P('sub', 'help'), may hold values from -6 to 6
- operator_panels: bfloat16 [384, 128, 1536], P(('sub', 'help')), may hold values from -1 to 4, as said below
- panel_index: int32 [384], P(('sub', 'help')), may hold values from 0 to 11, as said below
- halo_map: int32 [32, 512], P('sub'), may hold values from 0 to 1023, as said below
- counts: int32 [32], P('sub'), may hold values from 512 to 1024
Outputs:
- solution: float32 [32, 1024, 256], P('sub', 'help')
- residual: float32 [32, 1024, 256], P('sub', 'help')
Inputs may be any that keep to these rules, and one draw needn't show every extreme that they name: `panel_index`: within the 12 slots of one index of sub, every value appears exactly once. `halo_map`: the 512 entries of each subdomain are distinct; value v names row v of the subdomain of the previous index of sub. `operator_panels`: put in order, the 12 panels of each subdomain form a symmetric positive definite matrix.
All inputs are finite; a program needn't handle non-finite values.
Results may differ from a plain program's by a relative error of at most 0.023.
Values may be sent and summed in bfloat16 or wider, within the bound.
No kernel may reach another device: no remote copies, remote signals or barrier semaphores. Data moves between devices by JAX's collectives and lax.ppermute only.
A program may use at most 64 MiB of HBM per device.

v0:
```python
import jax
import jax.numpy as jnp
from jax import lax
from jax.sharding import Mesh
from jax.sharding import PartitionSpec as P

ITERS = 2
SUB = ("sub_0", "sub_1", "sub_2")
SUB_HELP = ("sub_0", "sub_1", "sub_2", "help")


def shifted(value, axis, by):
    devices = lax.axis_size(axis)
    pairs = [(i, i + by) for i in range(devices) if 0 <= i + by < devices]
    return lax.ppermute(value, axis, pairs)


def copy_for_each(value, axis):
    devices = lax.axis_size(axis)
    return lax.all_to_all(
        jnp.broadcast_to(value[None], (devices, *value.shape)), axis, 0, 0, tiled=True
    )


def laid_out(blocks, dim):
    lengths = list(blocks.shape[1:])
    lengths[dim] *= blocks.shape[0]
    return jnp.moveaxis(blocks, 0, dim).reshape(lengths)


def gathered_copies(value, axis, dim):
    blocks = copy_for_each(value, axis)
    return laid_out(blocks, dim)


def split_up(value, dim, devices):
    lengths = value.shape
    blocks = value.reshape(*lengths[:dim], devices, lengths[dim] // devices, *lengths[dim + 1 :])
    return jnp.moveaxis(blocks, dim, 0)


def sent_and_summed(value, axis, dim):
    blocks = split_up(value, dim, lax.axis_size(axis))
    arrived = lax.all_to_all(blocks, axis, split_axis=0, concat_axis=0, tiled=True)
    return arrived.astype(jnp.float32).sum(axis=0)


def sent_together(arrays, axis, dim, along):
    widths = [a.shape[along] for a in arrays]
    both = jnp.concatenate(arrays, axis=along)
    out = sent_and_summed(both, axis, dim)
    return tuple(jnp.split(out, [sum(widths[:k]) for k in range(1, len(widths))], axis=along))


def summed_on_arrival(value, axis, dim):
    blocks = split_up(value, dim, lax.axis_size(axis))
    arrived = lax.all_to_all(blocks, axis, split_axis=0, concat_axis=0, tiled=True)
    return arrived.sum(axis=0)


def sum_in_two_steps(value, axes, dim):
    far, near = axes
    blocks = split_up(value, dim, lax.axis_size(far))
    nearer = summed_on_arrival(blocks, near, dim + 1)
    arrived = lax.all_to_all(nearer, far, split_axis=0, concat_axis=0, tiled=True)
    return arrived.sum(axis=0)


def rows_for(lines, devices):
    spare = -len(lines) % devices
    return jnp.pad(lines, [(0, spare)] + [(0, 0)] * (lines.ndim - 1))


def whole_of(value, axes, dim):
    far, near = axes
    blocks = copy_for_each(copy_for_each(value, far), near)
    return laid_out(blocks.swapaxes(0, 1).reshape(-1, *value.shape), dim)


def total_of(value, axes):
    lines = value.reshape(-1, value.shape[-1])
    own = sum_in_two_steps(
        rows_for(lines, lax.axis_size(axes[0]) * lax.axis_size(axes[1])), axes, 0
    )
    whole = whole_of(own, axes, 0)
    return whole[: len(lines)].reshape(value.shape)


def spd_solve(matrix, targets):
    factor = jnp.linalg.cholesky(matrix)
    return jax.scipy.linalg.cho_solve((factor, True), targets)


def inner(left_block, right_block):
    column_count = left_block.shape[-1]
    return jnp.einsum(
        "nr,ns->rs",
        left_block.reshape(-1, column_count),
        right_block.reshape(-1, column_count),
        precision=lax.Precision.HIGHEST,
    )


def times(state_block, weights_mix):
    return jnp.dot(state_block, weights_mix, precision=lax.Precision.HIGHEST)


def shards(right_side, operator_panels, panel_index, halo_map, counts):
    domain_count, own_share, case_count = right_side.shape
    helpers = lax.axis_size("help")
    helper_id = lax.axis_index("help")
    owned_count = own_share * helpers
    halo_count = halo_map.shape[1]
    local_rows = owned_count + halo_count
    panel_rows = operator_panels.shape[1]
    per_domain = local_rows // panel_rows
    row_ids = helper_id * own_share + jnp.arange(own_share, dtype=jnp.int32)
    live_mask = (row_ids[None, :] < counts[:, None]).astype(jnp.float32)[:, :, None]
    flat_map = halo_map.reshape(-1)
    later_map = shifted(flat_map, SUB, -1)
    slot_domains = panel_index // per_domain
    residual = right_side * live_mask
    solution = jnp.zeros_like(residual)
    direction = residual
    norm_now = total_of(inner(residual, residual), (("sub_0", "sub_1"), ("sub_2", "help")))
    for iteration in range(ITERS):
        lowered = direction.astype(jnp.bfloat16)
        gathered = gathered_copies(lowered, "help", 1)
        owned_flat = gathered.reshape(domain_count * owned_count, case_count)
        picked_rows = jnp.take(owned_flat, later_map, axis=0)
        borrowed = shifted(picked_rows, SUB, 1)
        local_block = jnp.concatenate(
            [gathered, -borrowed.reshape(domain_count, halo_count, case_count)], axis=1
        )
        slot_blocks = jnp.take(local_block, slot_domains, axis=0)
        products = jnp.einsum(
            "spm,smc->spc", operator_panels, slot_blocks, preferred_element_type=jnp.float32
        ).astype(jnp.bfloat16)
        placed = (
            jnp.zeros((domain_count * per_domain, panel_rows, case_count), jnp.bfloat16)
            .at[panel_index]
            .set(products)
        )
        placed = placed.reshape(domain_count, local_rows, case_count)
        own_terms = placed[:, :owned_count].astype(jnp.float32)
        halo_terms = (
            placed[:, owned_count:]
            .astype(jnp.float32)
            .reshape(domain_count * halo_count, case_count)
        )
        back_terms = (
            jnp.zeros((domain_count * owned_count, case_count), jnp.float32)
            .at[flat_map]
            .add(-halo_terms)
        )
        back_terms = back_terms.reshape(domain_count, owned_count, case_count)
        at_home, for_before = sent_together(
            (own_terms.astype(jnp.bfloat16), back_terms.astype(jnp.bfloat16)), "help", 1, 0
        )
        returned = shifted(for_before.astype(jnp.bfloat16), SUB, -1)
        applied = (at_home + returned.astype(jnp.float32)) * live_mask
        curve, cross_term, square_term = (
            total_of(inner(direction, applied), (("sub_0", "sub_1"), ("sub_2", "help"))),
            total_of(inner(residual, applied), (("sub_0", "sub_1"), ("sub_2", "help"))),
            total_of(inner(applied, applied), (("sub_0", "sub_1"), ("sub_2", "help"))),
        )
        step_size = spd_solve(curve, norm_now)
        solution = solution + times(direction, step_size)
        residual = residual - times(applied, step_size)
        if iteration + 1 < ITERS:
            moved = times(cross_term, step_size)
            norm_next = (
                norm_now - moved - moved.T + times(step_size.T, times(square_term, step_size))
            )
            norm_next = 0.5 * (norm_next + norm_next.T)
            step_mix = spd_solve(norm_now, norm_next)
            direction = residual + times(direction, step_mix)
            norm_now = norm_next
    return (solution, residual)


def solution(mesh):
    torus = Mesh(
        mesh.devices.reshape(4, 4, 2, mesh.shape["help"]), ("sub_0", "sub_1", "sub_2", "help")
    )
    in_specs = (P(SUB, "help", None), P(SUB_HELP, None, None), P(SUB_HELP), P(SUB, None), P(SUB))
    out_specs = (P(SUB, "help", None), P(SUB, "help", None))
    return jax.shard_map(
        shards, mesh=torus, in_specs=in_specs, out_specs=out_specs, check_vma=False
    )
```

profile of v0, /device:TPU:1, one launch (start us, length us, event | category | flops | bytes accessed | tf_op | source)
XLA Modules:
  0.0 478.0 jit_solution(10427050795206733225)
XLA Ops:
  4.0 6.0 %all-to-all-start.6 = ((f32[8,16,2,256]{3,2,1,0:T(2,128)}), f32[8,16,2,256]{3,2,1,0:T(2,128)S(1)}, u32[]{:S(2)}, u32[]{:S(2)}) async-start(f32[8,16,2,256]{3,2,1,0:T(2,128)} %copy.153), calls=%async_computation.6 | async-start | bytes 524288 | tf_op jit(solution)/shard_map/all_to_all | solution.py:57
  12.0 4.5 all-to-all-done.6
  21.5 8.4 %all-to-all-done = bf16[4,1,256,256]{3,2,1,0:T(8,128)(2,1)S(1)} async-done(((bf16[4,1,256,256]{3,2,1,0:T(8,128)(2,1)}), bf16[4,1,256,256]{3,2,1,0:T(8,128)(2,1)S(1)}, u32[]{:S(2)}, u32[]{:S(2)}) %all-to-all-start) | async-done | bytes 524320 | tf_op jit(solution)/shard_map/all_to_all | solution.py:20
  30.0 7.6 %all-to-all-start.7 = ((f32[16,2,256]{2,1,0:T(2,128)}), f32[16,2,256]{2,1,0:T(2,128)S(1)}, u32[]{:S(2)}, u32[]{:S(2)}) async-start(f32[16,2,256]{2,1,0:T(2,128)} %reduce_sum.101), calls=%async_computation.7 | async-start | bytes 65536 | tf_op jit(solution)/shard_map/all_to_all | solution.py:65
  39.7 4.9 %collective-permute-start.1 = (bf16[512,256]{1,0:T(8,128)(2,1)S(1)}, bf16[512,256]{1,0:T(8,128)(2,1)S(1)}, u32[]{:S(2)}, u32[]{:S(2)}) collective-permute-start(bf16[512,256]{1,0:T(8,128)(2,1)S(1)} %broadcast_select_fusion.1), channel_id=1, source_target_pairs={{0,4},{4,8},{8,12},{12,16},{16,20},{20,24},{24,28},{28,32},{32,36}... | collective-permute-start | bytes 786440 | tf_op jit(solution)/shard_map/ppermute | solution.py:15
  45.9 6.2 %all-to-all-start.8 = ((f32[16,2,256]{2,1,0:T(2,128)}), f32[16,2,256]{2,1,0:T(2,128)S(1)}, u32[]{:S(2)}, u32[]{:S(2)}) async-start(f32[16,2,256]{2,1,0:T(2,128)} %broadcast_in_dim.49), calls=%async_computation.8 | async-start | bytes 65536 | tf_op jit(solution)/shard_map/all_to_all | solution.py:20
  52.1 6.7 %all-to-all-done.8 = f32[16,2,256]{2,1,0:T(2,128)S(1)} async-done(((f32[16,2,256]{2,1,0:T(2,128)}), f32[16,2,256]{2,1,0:T(2,128)S(1)}, u32[]{:S(2)}, u32[]{:S(2)}) %all-to-all-start.8) | async-done | bytes 32800 | tf_op jit(solution)/shard_map/all_to_all | solution.py:20
  59.6 4.3 all-to-all-start.9
  69.3 3.6 scatter_custom_fusion.1
  75.0 4.1 all-to-all-start.1
  81.0 12.6 %all-to-all-done.1 = bf16[4,2,256,256]{3,2,1,0:T(8,128)(2,1)S(1)} async-done(((bf16[4,2,256,256]{3,2,1,0:T(8,128)(2,1)}), bf16[4,2,256,256]{3,2,1,0:T(8,128)(2,1)S(1)}, u32[]{:S(2)}, u32[]{:S(2)}) %all-to-all-start.1) | async-done | bytes 1048608 | tf_op jit(solution)/shard_map/all_to_all | solution.py:44
  95.7 3.6 collective-permute-start.2
  99.4 11.7 %cholesky.206 = f32[128,128]{1,0:T(8,128)S(1)} custom-call(f32[128,128]{1,0:T(8,128)S(1)} %cholesky.273), custom_call_target="Cholesky" | custom-call | tf_op jit(solution)/shard_map/jit(cholesky)/cholesky | solution.py:90
  111.2 10.4 %custom-call.19 = f32[1,128,128]{1,2,0:T(8,128)} custom-call(f32[1,128,128]{2,1,0:T(8,128)S(1)} %get-tuple-element.78), custom_call_target="InvertDiagBlocksLowerTriangular" | custom-call | tf_op jit(solution)/shard_map/jit(cholesky)/cholesky | solution.py:90
  130.5 4.4 all-to-all-done.2
  134.9 3.7 all-to-all-start.10
  140.3 4.8 %all-to-all-done.10 = f32[8,16,2,256]{3,2,1,0:T(2,128)S(1)} async-done(((f32[8,16,2,256]{3,2,1,0:T(2,128)}), f32[8,16,2,256]{3,2,1,0:T(2,128)S(1)}, u32[]{:S(2)}, u32[]{:S(2)}) %all-to-all-start.10) | async-done | bytes 262176 | tf_op jit(solution)/shard_map/all_to_all | solution.py:57
  145.1 4.0 all-to-all-start.3
  150.3 11.7 %cholesky.223 = f32[128,128]{1,0:T(8,128)S(1)} custom-call(f32[128,128]{1,0:T(8,128)S(1)} %convolution_subtract_fusion.7), custom_call_target="Cholesky" | custom-call | tf_op jit(solution)/shard_map/jit(cholesky)/cholesky | solution.py:90
  162.7 6.8 %all-to-all-start.11 = ((f32[16,2,256]{2,1,0:T(2,128)}), f32[16,2,256]{2,1,0:T(2,128)S(1)}, u32[]{:S(2)}, u32[]{:S(2)}) async-start(f32[16,2,256]{2,1,0:T(2,128)} %reduce_sum.103), calls=%async_computation.11 | async-start | bytes 65536 | tf_op jit(solution)/shard_map/all_to_all | solution.py:65
  169.5 6.4 %all-to-all-done.11 = f32[16,2,256]{2,1,0:T(2,128)S(1)} async-done(((f32[16,2,256]{2,1,0:T(2,128)}), f32[16,2,256]{2,1,0:T(2,128)S(1)}, u32[]{:S(2)}, u32[]{:S(2)}) %all-to-all-start.11) | async-done | bytes 32800 | tf_op jit(solution)/shard_map/all_to_all | solution.py:65
  176.5 3.5 all-to-all-start.4
  182.0 4.5 all-to-all-done.4
  190.6 6.4 %all-to-all-done.12 = f32[16,2,256]{2,1,0:T(2,128)S(1)} async-done(((f32[16,2,256]{2,1,0:T(2,128)}), f32[16,2,256]{2,1,0:T(2,128)S(1)}, u32[]{:S(2)}, u32[]{:S(2)}) %all-to-all-start.12) | async-done | bytes 32800 | tf_op jit(solution)/shard_map/all_to_all | solution.py:20
  197.8 8.0 %all-to-all-start.5 = ((f32[8,16,2,256]{3,2,1,0:T(2,128)}), f32[8,16,2,256]{3,2,1,0:T(2,128)S(1)}, u32[]{:S(2)}, u32[]{:S(2)}) async-start(f32[8,16,2,256]{3,2,1,0:T(2,128)} %broadcast_in_dim.48), calls=%async_computation.5 | async-start | bytes 524288 | tf_op jit(solution)/shard_map/all_to_all | solution.py:20
  205.8 4.1 while.7
  209.9 20.3 %custom-call.20 = f32[2,128,128]{1,2,0:T(8,128)} custom-call(f32[2,128,128]{2,1,0:T(8,128)S(1)} %get-tuple-element.27), custom_call_target="InvertDiagBlocksLowerTriangular" | custom-call | tf_op jit(solution)/shard_map/jit(_cho_solve)/triangular_solve | solution.py:91
  231.0 5.3 %all-to-all-start.13 = ((f32[8,16,2,256]{3,2,1,0:T(2,128)}), f32[8,16,2,256]{3,2,1,0:T(2,128)}, u32[]{:S(2)}, u32[]{:S(2)}) async-start(f32[8,16,2,256]{3,2,1,0:T(2,128)} %broadcast_in_dim.52), calls=%async_computation.13 | async-start | bytes 524288 | tf_op jit(solution)/shard_map/all_to_all | solution.py:20
  237.4 11.7 %cholesky.172 = f32[128,128]{1,0:T(8,128)S(1)} custom-call(f32[128,128]{1,0:T(8,128)S(1)} %cholesky.270), custom_call_target="Cholesky" | custom-call | tf_op jit(solution)/shard_map/jit(cholesky)/cholesky | solution.py:90
  249.2 9.8 %custom-call.17 = f32[1,128,128]{1,2,0:T(8,128)S(1)} custom-call(f32[1,128,128]{2,1,0:T(8,128)S(1)} %get-tuple-element.82), custom_call_target="InvertDiagBlocksLowerTriangular" | custom-call | tf_op jit(solution)/shard_map/jit(cholesky)/cholesky | solution.py:90
  261.2 11.7 %cholesky.189 = f32[128,128]{1,0:T(8,128)S(1)} custom-call(f32[128,128]{1,0:T(8,128)S(1)} %convolution_subtract_fusion.8), custom_call_target="Cholesky" | custom-call | tf_op jit(solution)/shard_map/jit(cholesky)/cholesky | solution.py:90
  274.9 4.0 while.6
  278.9 19.8 %custom-call.18 = f32[2,128,128]{1,2,0:T(8,128)S(1)} custom-call(f32[2,128,128]{2,1,0:T(8,128)S(1)} %get-tuple-element.26), custom_call_target="InvertDiagBlocksLowerTriangular" | custom-call | tf_op jit(solution)/shard_map/jit(_cho_solve)/triangular_solve | solution.py:91
  308.4 12.6 %all_to_all.104 = bf16[4,1,256,256]{3,2,1,0:T(8,128)(2,1)S(1)} all-to-all(bf16[4,1,256,256]{3,2,1,0:T(8,128)(2,1)S(1)} %broadcast_in_dim.55), channel_id=1, replica_groups=mesh['sub_0'=4,'sub_1'=4,'sub_2'=2,'help'=4] {'help'}, dimensions={0} | all-to-all | bytes 1048576 | tf_op jit(solution)/shard_map/all_to_all | solution.py:20
  323.1 3.9 collective-permute-start.3
  336.5 4.0 scatter_custom_fusion.3
  341.6 15.3 %all_to_all.105 = bf16[4,2,256,256]{3,2,1,0:T(8,128)(2,1)S(1)} all-to-all(bf16[4,2,256,256]{3,2,1,0:T(8,128)(2,1)S(1)} %maximum_bitcast_fusion.1), channel_id=1, replica_groups=mesh['sub_0'=4,'sub_1'=4,'sub_2'=2,'help'=4] {'help'}, dimensions={0} | all-to-all | bytes 2097152 | tf_op jit(solution)/shard_map/all_to_all | solution.py:44
  359.5 5.8 %collective-permute-done.4 = bf16[1,256,256]{1,2,0:T(8,128)(2,1)S(1)} collective-permute-done((bf16[1,256,256]{1,2,0:T(8,128)(2,1)S(1)}, bf16[1,256,256]{1,2,0:T(8,128)(2,1)S(1)}, u32[]{:S(2)}, u32[]{:S(2)}) %collective-permute-start.4) | collective-permute-done | bytes 131104 | tf_op jit(solution)/shard_map/ppermute | solution.py:15
  365.8 8.9 %all_to_all.106 = f32[8,16,2,256]{3,2,1,0:T(2,128)S(1)} all-to-all(f32[8,16,2,256]{3,2,1,0:T(2,128)S(1)} %copy.175), channel_id=1, replica_groups=mesh['sub_0'=4,'sub_1'=4,'sub_2'=2,'help'=4] {'sub_2','help'}, dimensions={0} | all-to-all | bytes 524288 | tf_op jit(solution)/shard_map/all_to_all | solution.py:57
  374.8 13.9 %all_to_all.107 = f32[16,2,256]{2,1,0:T(2,128)S(1)} all-to-all(f32[16,2,256]{2,1,0:T(2,128)S(1)} %reduce_sum.106), channel_id=1, replica_groups=mesh['sub_0'=4,'sub_1'=4,'sub_2'=2,'help'=4] {'sub_0','sub_1'}, dimensions={0} | all-to-all | bytes 65536 | tf_op jit(solution)/shard_map/all_to_all | solution.py:65
  388.7 9.6 %all_to_all.108 = f32[16,2,256]{2,1,0:T(2,128)S(1)} all-to-all(f32[16,2,256]{2,1,0:T(2,128)S(1)} %broadcast_in_dim.56), channel_id=1, replica_groups=mesh['sub_0'=4,'sub_1'=4,'sub_2'=2,'help'=4] {'sub_0','sub_1'}, dimensions={0} | all-to-all | bytes 65536 | tf_op jit(solution)/shard_map/all_to_all | solution.py:20
  399.0 6.5 %all-to-all-start.19 = ((f32[8,16,2,256]{3,2,1,0:T(2,128)}), f32[8,16,2,256]{3,2,1,0:T(2,128)S(1)}, u32[]{:S(2)}, u32[]{:S(2)}) async-start(f32[8,16,2,256]{3,2,1,0:T(2,128)} %broadcast_in_dim.57), calls=%async_computation.19 | async-start | bytes 524288 | tf_op jit(solution)/shard_map/all_to_all | solution.py:20
  406.1 5.9 %all-to-all-done.19 = f32[8,16,2,256]{3,2,1,0:T(2,128)S(1)} async-done(((f32[8,16,2,256]{3,2,1,0:T(2,128)}), f32[8,16,2,256]{3,2,1,0:T(2,128)S(1)}, u32[]{:S(2)}, u32[]{:S(2)}) %all-to-all-start.19) | async-done | bytes 262176 | tf_op jit(solution)/shard_map/all_to_all | solution.py:20
  412.5 11.7 %cholesky.240 = f32[128,128]{1,0:T(8,128)S(1)} custom-call(f32[128,128]{1,0:T(8,128)S(1)} %cholesky.276), custom_call_target="Cholesky" | custom-call | tf_op jit(solution)/shard_map/jit(cholesky)/cholesky | solution.py:90
  424.3 9.8 %custom-call.21 = f32[1,128,128]{1,2,0:T(8,128)S(1)} custom-call(f32[1,128,128]{2,1,0:T(8,128)S(1)} %get-tuple-element.74), custom_call_target="InvertDiagBlocksLowerTriangular" | custom-call | tf_op jit(solution)/shard_map/jit(cholesky)/cholesky | solution.py:90
  434.6 11.7 %cholesky.257 = f32[128,128]{1,0:T(8,128)S(1)} custom-call(f32[128,128]{1,0:T(8,128)S(1)} %convolution_subtract_fusion.6), custom_call_target="Cholesky" | custom-call | tf_op jit(solution)/shard_map/jit(cholesky)/cholesky | solution.py:90
  449.0 4.0 while.8
  453.0 19.9 %custom-call.22 = f32[2,128,128]{1,2,0:T(8,128)S(1)} custom-call(f32[2,128,128]{2,1,0:T(8,128)S(1)} %get-tuple-element.28), custom_call_target="InvertDiagBlocksLowerTriangular" | custom-call | tf_op jit(solution)/shard_map/jit(_cho_solve)/triangular_solve | solution.py:91
  (218 shorter events, 94.1 us)
Async XLA Ops:
  0.6 64.5 %copy-start = (bf16[3,128,1536]{2,1,0:T(8,128)(2,1)S(1)}, bf16[3,128,1536]{2,1,0:T(8,128)(2,1)}, u32[]{:S(2)}) copy-start(bf16[3,128,1536]{2,1,0:T(8,128)(2,1)} %param.13) | copy-start | bytes 3538948
  2.5 7.4 %copy-start.10 = (s32[1,512]{1,0:T(1,128)S(1)}, s32[1,512]{1,0:T(1,128)}, u32[]{:S(2)}) copy-start(s32[1,512]{1,0:T(1,128)} %param.15) | copy-start | bytes 6148
  4.0 12.5 %all-to-all-start.6 = ((f32[8,16,2,256]{3,2,1,0:T(2,128)}), f32[8,16,2,256]{3,2,1,0:T(2,128)S(1)}, u32[]{:S(2)}, u32[]{:S(2)}) async-start(f32[8,16,2,256]{3,2,1,0:T(2,128)} %copy.153), calls=%async_computation.6 | async-start | bytes 524288 | tf_op jit(solution)/shard_map/all_to_all | solution.py:57
  9.9 10.8 %collective-permute-start = (s32[512]{0:T(512)S(1)}, s32[512]{0:T(512)S(1)}, u32[]{:S(2)}, u32[]{:S(2)}) collective-permute-start(s32[512]{0:T(512)S(1)} %bitcast.241), channel_id=1, source_target_pairs={{4,0},{8,4},{12,8},{16,12},{20,16},{24,20},{28,24},{32,28},{36,32}... | collective-permute-start | bytes 6152 | tf_op jit(solution)/shard_map/ppermute | solution.py:15
  11.9 57.4 %copy-start.11 = (s32[512,1]{0,1:T(1,128)}, s32[512,1]{0,1:T(1,128)S(1)}, u32[]{:S(2)}) copy-start(s32[512,1]{0,1:T(1,128)S(1)} %compare_select_fusion) | copy-start | bytes 6148
  17.3 12.7 %all-to-all-start = ((bf16[4,1,256,256]{3,2,1,0:T(8,128)(2,1)}), bf16[4,1,256,256]{3,2,1,0:T(8,128)(2,1)S(1)}, u32[]{:S(2)}, u32[]{:S(2)}) async-start(bf16[4,1,256,256]{3,2,1,0:T(8,128)(2,1)} %broadcast_in_dim.46), calls=%async_computation | async-start | bytes 1048576 | tf_op jit(solution)/shard_map/all_to_all | solution.py:20
  30.0 15.2 %all-to-all-start.7 = ((f32[16,2,256]{2,1,0:T(2,128)}), f32[16,2,256]{2,1,0:T(2,128)S(1)}, u32[]{:S(2)}, u32[]{:S(2)}) async-start(f32[16,2,256]{2,1,0:T(2,128)} %reduce_sum.101), calls=%async_computation.7 | async-start | bytes 65536 | tf_op jit(solution)/shard_map/all_to_all | solution.py:65
  37.6 7.0 %copy-start.14 = (s32[3]{0:T(128)S(1)}, s32[3]{0:T(128)}, u32[]{:S(2)}) copy-start(s32[3]{0:T(128)} %param.14) | copy-start | bytes 40
  39.7 24.2 %collective-permute-start.1 = (bf16[512,256]{1,0:T(8,128)(2,1)S(1)}, bf16[512,256]{1,0:T(8,128)(2,1)S(1)}, u32[]{:S(2)}, u32[]{:S(2)}) collective-permute-start(bf16[512,256]{1,0:T(8,128)(2,1)S(1)} %broadcast_select_fusion.1), channel_id=1, source_target_pairs={{0,4},{4,8},{8,12},{12,16},{16,20},{20,24},{24,28},{28,32},{32,36}... | collective-permute-start | bytes 786440 | tf_op jit(solution)/shard_map/ppermute | solution.py:15
  45.9 13.0 %all-to-all-start.8 = ((f32[16,2,256]{2,1,0:T(2,128)}), f32[16,2,256]{2,1,0:T(2,128)S(1)}, u32[]{:S(2)}, u32[]{:S(2)}) async-start(f32[16,2,256]{2,1,0:T(2,128)} %broadcast_in_dim.49), calls=%async_computation.8 | async-start | bytes 65536 | tf_op jit(solution)/shard_map/all_to_all | solution.py:20
  52.1 13.1 %copy-start.16 = (pred[3]{0:T(512)(128)(4,1)}, pred[3]{0:T(512)(128)(4,1)S(1)}, u32[]{:S(2)}) copy-start(pred[3]{0:T(512)(128)(4,1)S(1)} %compare_and_fusion) | copy-start | bytes 13
  59.6 15.4 %all-to-all-start.9 = ((f32[8,16,2,256]{3,2,1,0:T(2,128)}), f32[8,16,2,256]{3,2,1,0:T(2,128)}, u32[]{:S(2)}, u32[]{:S(2)}) async-start(f32[8,16,2,256]{3,2,1,0:T(2,128)} %broadcast_in_dim.50), calls=%async_computation.9 | async-start | bytes 524288 | tf_op jit(solution)/shard_map/all_to_all | solution.py:20
  67.1 0.7 copy-start.12
  72.9 1.0 copy-start.5
  75.0 18.7 %all-to-all-start.1 = ((bf16[4,2,256,256]{3,2,1,0:T(8,128)(2,1)}), bf16[4,2,256,256]{3,2,1,0:T(8,128)(2,1)S(1)}, u32[]{:S(2)}, u32[]{:S(2)}) async-start(bf16[4,2,256,256]{3,2,1,0:T(8,128)(2,1)} %maximum_bitcast_fusion), calls=%async_computation.1 | async-start | bytes 2097152 | tf_op jit(solution)/shard_map/all_to_all | solution.py:44
  95.7 28.7 %collective-permute-start.2 = (bf16[1,256,256]{1,2,0:T(8,128)(2,1)S(1)}, bf16[1,256,256]{1,2,0:T(8,128)(2,1)S(1)}, u32[]{:S(2)}, u32[]{:S(2)}) collective-permute-start(bf16[1,256,256]{1,2,0:T(8,128)(2,1)S(1)} %copy.201), channel_id=1, source_target_pairs={{4,0},{8,4},{12,8},{16,12},{20,16},{24,20},{28,24},{32,28},{36,32}... | collective-permute-start | bytes 393224 | tf_op jit(solution)/shard_map/ppermute | solution.py:15
  99.4 26.3 %copy-start.6 = (f32[256,256]{1,0:T(8,128)}, f32[256,256]{1,0:T(8,128)S(1)}, u32[]{:S(2)}) copy-start(f32[256,256]{1,0:T(8,128)S(1)} %fusion.49) | copy-start | bytes 786436
  125.6 9.3 %all-to-all-start.2 = ((f32[8,16,2,256]{3,2,1,0:T(2,128)}), f32[8,16,2,256]{3,2,1,0:T(2,128)S(1)}, u32[]{:S(2)}, u32[]{:S(2)}) async-start(f32[8,16,2,256]{3,2,1,0:T(2,128)} %copy.147), calls=%async_computation.2 | async-start | bytes 524288 | tf_op jit(solution)/shard_map/all_to_all | solution.py:57
  129.0 9.5 %copy-start.9 = (f32[1,128,128]{1,2,0:T(8,128)S(1)}, f32[1,128,128]{1,2,0:T(8,128)}, u32[]{:S(2)}) copy-start(f32[1,128,128]{1,2,0:T(8,128)} %custom-call.19) | copy-start | bytes 196612
  134.9 10.2 %all-to-all-start.10 = ((f32[8,16,2,256]{3,2,1,0:T(2,128)}), f32[8,16,2,256]{3,2,1,0:T(2,128)S(1)}, u32[]{:S(2)}, u32[]{:S(2)}) async-start(f32[8,16,2,256]{3,2,1,0:T(2,128)} %copy.161), calls=%async_computation.10 | async-start | bytes 524288 | tf_op jit(solution)/shard_map/all_to_all | solution.py:57
  145.1 17.6 %all-to-all-start.3 = ((f32[16,2,256]{2,1,0:T(2,128)}), f32[16,2,256]{2,1,0:T(2,128)S(1)}, u32[]{:S(2)}, u32[]{:S(2)}) async-start(f32[16,2,256]{2,1,0:T(2,128)} %reduce_sum.99), calls=%async_computation.3 | async-start | bytes 65536 | tf_op jit(solution)/shard_map/all_to_all | solution.py:65
  149.1 56.6 %copy-start.15 = (s32[2]{0:T(128)S(1)}, s32[2]{0:T(128)}, u32[]{:S(2)}) copy-start(s32[2]{0:T(128)} %iota_multiply_fusion) | copy-start | bytes 28
  162.7 13.2 %all-to-all-start.11 = ((f32[16,2,256]{2,1,0:T(2,128)}), f32[16,2,256]{2,1,0:T(2,128)S(1)}, u32[]{:S(2)}, u32[]{:S(2)}) async-start(f32[16,2,256]{2,1,0:T(2,128)} %reduce_sum.103), calls=%async_computation.11 | async-start | bytes 65536 | tf_op jit(solution)/shard_map/all_to_all | solution.py:65
  176.5 9.9 %all-to-all-start.4 = ((f32[16,2,256]{2,1,0:T(2,128)}), f32[16,2,256]{2,1,0:T(2,128)S(1)}, u32[]{:S(2)}, u32[]{:S(2)}) async-start(f32[16,2,256]{2,1,0:T(2,128)} %broadcast_in_dim.47), calls=%async_computation.4 | async-start | bytes 65536 | tf_op jit(solution)/shard_map/all_to_all | solution.py:20
  187.1 9.9 %all-to-all-start.12 = ((f32[16,2,256]{2,1,0:T(2,128)}), f32[16,2,256]{2,1,0:T(2,128)S(1)}, u32[]{:S(2)}, u32[]{:S(2)}) async-start(f32[16,2,256]{2,1,0:T(2,128)} %broadcast_in_dim.51), calls=%async_computation.12 | async-start | bytes 65536 | tf_op jit(solution)/shard_map/all_to_all | solution.py:20
  197.8 32.4 %all-to-all-start.5 = ((f32[8,16,2,256]{3,2,1,0:T(2,128)}), f32[8,16,2,256]{3,2,1,0:T(2,128)S(1)}, u32[]{:S(2)}, u32[]{:S(2)}) async-start(f32[8,16,2,256]{3,2,1,0:T(2,128)} %broadcast_in_dim.48), calls=%async_computation.5 | async-start | bytes 524288 | tf_op jit(solution)/shard_map/all_to_all | solution.py:20
  231.0 69.5 %all-to-all-start.13 = ((f32[8,16,2,256]{3,2,1,0:T(2,128)}), f32[8,16,2,256]{3,2,1,0:T(2,128)}, u32[]{:S(2)}, u32[]{:S(2)}) async-start(f32[8,16,2,256]{3,2,1,0:T(2,128)} %broadcast_in_dim.52), calls=%async_computation.13 | async-start | bytes 524288 | tf_op jit(solution)/shard_map/all_to_all | solution.py:20
  236.7 0.7 copy-start.7
  303.3 1.8 copy-start.8
  307.6 0.7 copy-start.2
  323.1 7.2 %collective-permute-start.3 = (bf16[512,256]{1,0:T(8,128)(2,1)S(1)}, bf16[512,256]{1,0:T(8,128)(2,1)S(1)}, u32[]{:S(2)}, u32[]{:S(2)}) collective-permute-start(bf16[512,256]{1,0:T(8,128)(2,1)S(1)} %broadcast_select_fusion), channel_id=1, source_target_pairs={{0,4},{4,8},{8,12},{12,16},{16,20},{20,24},{24,28},{28,32},{32,36}... | collective-permute-start | bytes 786440 | tf_op jit(solution)/shard_map/ppermute | solution.py:15
  330.3 1.2 copy-start.17
  333.4 0.7 copy-start.13
  334.8 0.9 copy-start.1
  340.5 1.0 copy-start.4
  357.2 8.0 %collective-permute-start.4 = (bf16[1,256,256]{1,2,0:T(8,128)(2,1)S(1)}, bf16[1,256,256]{1,2,0:T(8,128)(2,1)S(1)}, u32[]{:S(2)}, u32[]{:S(2)}) collective-permute-start(bf16[1,256,256]{1,2,0:T(8,128)(2,1)S(1)} %copy.203), channel_id=1, source_target_pairs={{4,0},{8,4},{12,8},{16,12},{20,16},{24,20},{28,24},{32,28},{36,32}... | collective-permute-start | bytes 393224 | tf_op jit(solution)/shard_map/ppermute | solution.py:15
  399.0 13.0 %all-to-all-start.19 = ((f32[8,16,2,256]{3,2,1,0:T(2,128)}), f32[8,16,2,256]{3,2,1,0:T(2,128)S(1)}, u32[]{:S(2)}, u32[]{:S(2)}) async-start(f32[8,16,2,256]{3,2,1,0:T(2,128)} %broadcast_in_dim.57), calls=%async_computation.19 | async-start | bytes 524288 | tf_op jit(solution)/shard_map/all_to_all | solution.py:20
  473.6 2.5 copy-start.3
where the time goes:
time: 486 us; the launch traced here: 478 us
  other arithmetic  177 us (36%)
  starting transfers between devices  92.5 us (19%)
  waiting for transfers between devices  73.8 us (15%)
  blocking collectives  60.2 us (12%)
  local copies, waits for them, and re-layouts  44.8 us (9%)
  matrix products  22.4 us (5%)
  between operations  6.73 us (1%)
    another operation x19, other arithmetic, spd_solve(): factor = jnp.linalg.cholesky(matrix)  103 us
    another operation x7, other arithmetic, spd_solve(): return jax.scipy.linalg.cho_solve((factor, True), targets)  60.7 us
    all_to_all x8, starting transfers between devices, copy_for_each(): lax.all_to_all(jnp.broadcast_to(value[None], (devices, *value.shape)), ax...  40.7 us
    all_to_all x8, waiting for transfers between devices, copy_for_each(): lax.all_to_all(jnp.broadcast_to(value[None], (devices, *value.shape)), ax...  32 us
    all_to_all x2, blocking collectives, copy_for_each(): lax.all_to_all(jnp.broadcast_to(value[None], (devices, *value.shape)), ax...  22.1 us
    all_to_all x3, starting transfers between devices, sum_in_two_steps(): lax.all_to_all(nearer, far, split_axis=0, concat_axis=0, tiled=True)  18.4 us
    ppermute x5, starting transfers between devices, shifted(): return lax.ppermute(value, axis, pairs)  16.3 us
    all_to_all x1, blocking collectives, sent_and_summed(): lax.all_to_all(blocks, axis, split_axis=0, concat_axis=0, tiled=True)  15.3 us
  transfers between devices with their start and end apart: 20, of which 12 were waited for; matrix products, arithmetic and copies ran while one was open for 31% of the time, Pallas kernels for 0%

commit v1 on v0

v1 whole, which is shorter than its diff:
```python
import jax
import jax.numpy as jnp
from jax import lax
from jax.experimental import pallas as pl
from jax.experimental.pallas import tpu as pltpu
from jax.sharding import Mesh
from jax.sharding import PartitionSpec as P

SUB = ("sub_0", "sub_1", "sub_2")
SUB_HELP = ("sub_0", "sub_1", "sub_2", "help")
SHIFT = 3.0
BF = jnp.bfloat16
F32 = jnp.float32


def shifted(value, axis, by):
    devices = lax.axis_size(axis)
    pairs = [(i, i + by) for i in range(devices) if 0 <= i + by < devices]
    return lax.ppermute(value, axis, pairs)


def turned(value, axis, by):
    devices = lax.axis_size(axis)
    return lax.ppermute(value, axis, [(i, (i + by) % devices) for i in range(devices)])


def from_others(value, axis):
    return [turned(value, axis, by) for by in range(1, lax.axis_size(axis))]


def summed(value, axis):
    total = value
    for other in from_others(value, axis):
        total = total + other
    return total


def whole(space=None):
    return pl.BlockSpec(memory_space=pltpu.MemorySpace.VMEM if space is None else space)


def scalars():
    return pl.BlockSpec(memory_space=pltpu.MemorySpace.SMEM)


def call(body, args, outs, scratch=(), small=1, name=None):
    specs = [scalars()] * small + [whole()] * (len(args) - small)
    return pl.pallas_call(
        body,
        in_specs=specs,
        out_specs=[whole() for _ in outs],
        out_shape=[jax.ShapeDtypeStruct(s, d) for s, d in outs],
        scratch_shapes=list(scratch),
        name=name,
    )(*args)


def iota(shape, dim):
    return lax.broadcasted_iota(jnp.int32, shape, dim)


def mm(a, b):
    return lax.dot_general(a, b, (((1,), (0,)), ((), ())), preferred_element_type=F32)


def tmm(a, b):
    return lax.dot_general(a, b, (((0,), (0,)), ((), ())), preferred_element_type=F32)


def halves(a):
    high = a.astype(BF)
    return high, (a - high.astype(F32)).astype(BF)


def mm3(a, b):
    ah, al = halves(a)
    bh, bl = halves(b)
    return mm(ah, bh) + (mm(ah, bl) + mm(al, bh))


def mmf(a, b):
    return jnp.dot(a, b, precision=lax.Precision.HIGHEST, preferred_element_type=F32)


def hot(mask):
    return jnp.where(mask, 1.0, 0.0).astype(BF)


def lower_body(sc, r_ref, out_ref):
    rows = r_ref.shape[0]
    cols = r_ref.shape[1]
    row = iota((rows, 1), 0) + sc[0] * rows
    live = row < sc[1]
    out_ref[:rows, :] = jnp.where(live, r_ref[...], 0.0).astype(BF)
    col = iota((16, cols), 1)
    info = jnp.zeros((16, cols), F32)
    values = [sc[3], sc[4], sc[5], sc[1] // 32, sc[1] % 32]
    for k, value in enumerate(values):
        info = jnp.where(col == k, value.astype(F32), info)
    out_ref[rows:, :] = info.astype(BF)


def pick_body(sc, own_ref, a_ref, b_ref, c_ref, later_ref, wg_ref, pick_ref):
    rows = own_ref.shape[0] - 16
    h = sc[0]
    for k, ref in enumerate((own_ref, a_ref, b_ref, c_ref)):
        at = pl.multiple_of(lax.rem(h + 4 - k, 4) * rows, rows)
        wg_ref[pl.ds(at, rows), :] = ref[:rows, :]
    halo = later_ref.shape[0]
    choose = hot(later_ref[...] == iota((halo, wg_ref.shape[0]), 1))
    pick_ref[:halo, :] = mm(choose, wg_ref[...]).astype(BF)
    pick_ref[halo:, :] = own_ref[rows:, :]


def first_body(f_ref, wg_ref, halo_ref, z_ref):
    owned = wg_ref.shape[0]
    halo = f_ref.shape[1] - owned
    z = mm(f_ref[:, :owned], wg_ref[...]) - mm(f_ref[:, owned:], halo_ref[:halo, :])
    z_ref[...] = z.astype(BF)


def spread_body(sc, own_ref, a_ref, b_ref, c_ref, later_ref, zg_ref, halo_ref, pick_ref):
    panel = own_ref.shape[0] // 3
    for k, ref in enumerate((own_ref, a_ref, b_ref, c_ref)):
        for j in range(3):
            at = pl.multiple_of(sc[3 + 3 * k + j] * panel, panel)
            zg_ref[pl.ds(at, panel), :] = ref[j * panel : (j + 1) * panel, :]
    halo = halo_ref.shape[0]
    owned = zg_ref.shape[0] - halo
    halo_ref[...] = zg_ref[owned:, :]
    later = later_ref[...]
    choose = hot((later == iota((halo, owned), 1)) & (later < sc[1]))
    pick_ref[...] = mm(choose, zg_ref[:owned, :]).astype(BF)


def second_body(
    sc, f_ref, zg_ref, ret_ref, zp_ref, bor_ref, wg_ref, map_ref, later_ref, z_ref, im_ref, vb_ref, vh_ref
):
    owned = wg_ref.shape[0]
    halo = ret_ref.shape[0]
    live = iota((owned, 1), 0) < sc[1]
    back = mm(hot(iota((owned, halo), 0) == later_ref[...]), ret_ref[...])
    image = jnp.where(live, zg_ref[:owned, :].astype(F32) - back, 0.0)
    im_ref[...] = image
    vb = (image - SHIFT * wg_ref[...].astype(F32)).astype(BF)
    vb_ref[...] = vb
    info = bor_ref[halo : halo + 1, :].astype(F32)
    lane = iota(info.shape, 1)
    weight = jnp.where(lane == 3, 32.0, jnp.where(lane == 4, 1.0, 0.0))
    count = jnp.sum(info * weight, axis=1, keepdims=True)
    alive = (map_ref[...].astype(F32) < count) & (sc[2] > 0)
    term = zp_ref[...].astype(F32) - zg_ref[owned:, :].astype(F32)
    vh = jnp.where(alive, term, 0.0) - SHIFT * bor_ref[:halo, :].astype(F32)
    vh = vh.astype(BF)
    vh_ref[...] = vh
    z = mm(f_ref[:, :owned], vb) - mm(f_ref[:, owned:], vh)
    z_ref[...] = z.astype(BF)


def gram_body(
    sc, own_ref, a_ref, b_ref, c_ref, wg_ref, bor_ref, zg_ref, im_ref, vb_ref, vh_ref, map_ref,
    pack_ref, back_ref, mine_ref, z2_ref, gram_ref,
):
    panel = own_ref.shape[0] // 3
    for k, ref in enumerate((own_ref, a_ref, b_ref, c_ref)):
        for j in range(3):
            at = pl.multiple_of(sc[3 + 3 * k + j] * panel, panel)
            z2_ref[pl.ds(at, panel), :] = ref[j * panel : (j + 1) * panel, :]
    owned = wg_ref.shape[0]
    halo = vh_ref.shape[0]
    rows = mine_ref.shape[0]
    h = sc[0]
    at = pl.multiple_of(h * rows, rows)
    mine_ref[...] = z2_ref[pl.ds(at, rows), :]
    choose = hot(iota((rows, halo), 0) + h * rows == map_ref[...])
    back_ref[...] = mm(choose, z2_ref[owned:, :]).astype(BF)

    @pl.when(h == 0)
    def _():
        gram_ref[...] = tmm(wg_ref[...], wg_ref[...])

    @pl.when(h == 1)
    def _():
        gram_ref[...] = tmm(wg_ref[...], zg_ref[:owned, :]) - tmm(bor_ref[:halo, :], zg_ref[owned:, :])

    @pl.when(h == 2)
    def _():
        high, low = halves(im_ref[...])
        cross = tmm(low, high)
        gram_ref[...] = tmm(high, high) + (cross + cross.T)

    @pl.when(h == 3)
    def _():
        gram_ref[...] = tmm(vb_ref[...], z2_ref[:owned, :]) - tmm(vh_ref[...], z2_ref[owned:, :])

    half = gram_ref.shape[0] // 2
    lower = gram_ref[:half, :half]
    upper = gram_ref[half:, half:]
    r, c = iota((half, half), 0), iota((half, half), 1)
    pack_ref[:half, :] = jnp.where(r >= c, lower, upper.T)
    pack_ref[half : 2 * half, :] = gram_ref[half:, :half]
    diagonal = jnp.sum(jnp.where(r == c, upper, 0.0), axis=0, keepdims=True)
    pack_ref[2 * half :, :] = jnp.broadcast_to(diagonal, (8, half))


def unpacked(pack, out_ref):
    half = pack.shape[1]
    r, c = iota((half, half), 0), iota((half, half), 1)
    both = pack[:half, :]
    flip = both.T
    side = pack[half : 2 * half, :]
    out_ref[:half, :half] = jnp.where(r >= c, both, flip)
    out_ref[half:, half:] = jnp.where(r == c, pack[2 * half : 2 * half + 1, :], jnp.where(r < c, both, flip))
    out_ref[half:, :half] = side
    out_ref[:half, half:] = side.T


def inverse(k, x_ref):
    n = k.shape[0]
    r, c = iota((n, n), 0), iota((n, n), 1)
    eye = jnp.where(r == c, 1.0, 0.0)
    on = jnp.where(r == c, k, 0.0)
    by_row = lax.rsqrt(jnp.sum(on, axis=1, keepdims=True))
    by_col = lax.rsqrt(jnp.sum(on, axis=0, keepdims=True))
    unit = k * by_row * by_col
    norm = jnp.max(jnp.sum(jnp.abs(unit), axis=0, keepdims=True), axis=1, keepdims=True)
    step = 2.0 / (1.0 + norm)
    x_ref[...] = step * (2.0 * eye - step * unit)

    def more(state):
        return (state[0] < 60) & (state[1] > 1e-3)

    def improve(state):
        x = x_ref[...]
        left = eye - mmf(unit, x)
        x_ref[...] = x + mmf(x, left)
        return state[0] + 1, jnp.max(jnp.sum(jnp.abs(left), axis=0, keepdims=True))

    lax.while_loop(more, improve, (jnp.int32(0), jnp.float32(1.0)))
    return x_ref[...] * by_row * by_col


def solve_body(
    sc, own_ref, a_ref, b_ref, c_ref, r_ref, im_ref, w_ref, mine_ref, ret_ref,
    sol_ref, res_ref, pack_ref, g00_ref, g01_ref, g11_ref, gvv_ref, x_ref,
):
    h = sc[0]
    for k, ref in enumerate((own_ref, a_ref, b_ref, c_ref)):
        pack_ref[lax.rem(h + 4 - k, 4)] = ref[...]
    for k, ref in enumerate((g00_ref, g01_ref, g11_ref, gvv_ref)):
        unpacked(pack_ref[k], ref)
    g01 = g01_ref[...]
    mixed = g11_ref[...] - SHIFT * g01
    inv = inverse(g01, x_ref)
    p1 = mmf(inv, mixed)
    p2 = mmf(inv, g00_ref[...])
    schur = gvv_ref[...] - mmf(mixed, p1)
    schur = 0.5 * (schur + schur.T)
    rest = g01 - SHIFT * g00_ref[...] - mmf(mixed, p2)
    cv = mmf(inverse(schur, x_ref), rest)
    cr = p2 - mmf(p1, cv)
    rows = r_ref.shape[0]
    live = iota((rows, 1), 0) + h * rows < sc[1]
    r = jnp.where(live, r_ref[...], 0.0)
    at = pl.multiple_of(h * rows, rows)
    im = im_ref[pl.ds(at, rows), :]
    v = im - SHIFT * w_ref[:rows, :].astype(F32)
    av = jnp.where(live, mine_ref[...].astype(F32) - ret_ref[...].astype(F32), 0.0)
    sol_ref[...] = mm3(r, cr) + mm3(v, cv)
    res_ref[...] = r - mm3(im, cr) - mm3(av, cv)


def shards(right_side, operator_panels, panel_index, halo_map, counts):
    rows, cols = right_side.shape[1:]
    slots, panel, wide = operator_panels.shape
    halo = halo_map.shape[1]
    owned = rows * lax.axis_size("help")
    helper = lax.axis_index("help").astype(jnp.int32)
    group = lax.axis_index(SUB).astype(jnp.int32)
    r = right_side.reshape(rows, cols)
    f = operator_panels.reshape(slots * panel, wide)
    head = jnp.stack([helper, counts[0], (group > 0).astype(jnp.int32)])
    sc = jnp.concatenate([head, panel_index])
    later = shifted(halo_map.reshape(halo), SUB, -1)
    later_col, later_row = later.reshape(halo, 1), later.reshape(1, halo)
    map_col, map_row = halo_map.reshape(halo, 1), halo_map.reshape(1, halo)

    (low,) = call(lower_body, (sc, r), [((rows + 16, cols), BF)], name="lower")
    others = from_others(low, "help")
    tables = [o[rows, :slots].astype(jnp.int32) for o in others]
    sc = jnp.concatenate([sc, *tables])
    wg, pick = call(
        pick_body, (sc, low, *others, later_col), [((owned, cols), BF), ((halo + 16, cols), BF)], name="pick"
    )
    bor = shifted(pick, SUB, 1)
    (z,) = call(first_body, (f, wg, bor), [((slots * panel, cols), BF)], small=0, name="first")
    zs = from_others(z, "help")
    zg, zh, zpick = call(
        spread_body,
        (sc, z, *zs, later_col),
        [((wide, cols), BF), ((halo, cols), BF), ((halo, cols), BF)],
        name="spread",
    )
    ret = shifted(zh, SUB, -1)
    zp = shifted(zpick, SUB, 1)
    z2, im, vb, vh = call(
        second_body,
        (sc, f, zg, ret, zp, bor, wg, map_col, later_row),
        [((slots * panel, cols), BF), ((owned, cols), F32), ((owned, cols), BF), ((halo, cols), BF)],
        name="second",
    )
    z2s = from_others(z2, "help")
    pack, back, mine = call(
        gram_body,
        (sc, z2, *z2s, wg, bor, zg, im, vb, vh, map_row),
        [((cols + 8, cols // 2), F32), ((rows, cols), BF), ((rows, cols), BF)],
        scratch=[pltpu.VMEM((wide, cols), BF), pltpu.VMEM((cols, cols), F32)],
        name="gram",
    )
    ret2 = shifted(back, SUB, -1)
    pack = summed(pack, "sub_2")
    pack = summed(pack, "sub_0")
    pack = summed(pack, "sub_1")
    packs = from_others(pack, "help")
    sol, res = call(
        solve_body,
        (sc, pack, *packs, r, im, low, mine, ret2),
        [((rows, cols), F32), ((rows, cols), F32)],
        scratch=[pltpu.VMEM((4, cols + 8, cols // 2), F32)] + [pltpu.VMEM((cols, cols), F32)] * 5,
        name="solve",
    )
    return sol.reshape(right_side.shape), res.reshape(right_side.shape)


def solution(mesh):
    torus = Mesh(
        mesh.devices.reshape(4, 4, 2, mesh.shape["help"]), ("sub_0", "sub_1", "sub_2", "help")
    )
    in_specs = (P(SUB, "help", None), P(SUB_HELP, None, None), P(SUB_HELP), P(SUB, None), P(SUB))
    out_specs = (P(SUB, "help", None), P(SUB, "help", None))
    return jax.shard_map(
        shards, mesh=torus, in_specs=in_specs, out_specs=out_specs, check_vma=False
    )
```

time: 486 us -> 147 us (0.30); the launches traced: 478 us -> 147 us
  other arithmetic: 177 us -> 2.27 us
  blocking collectives: 60.2 us -> 0 us
  starting transfers between devices: 92.5 us -> 41.2 us
  Pallas kernels: 0 us -> 43.1 us
  local copies, waits for them, and re-layouts: 44.8 us -> 6.5 us
  matrix products: 22.4 us -> 0 us
  waiting for transfers between devices: 73.8 us -> 52.1 us
  between operations: 6.73 us -> 1.43 us
    another operation x26 -> x0, other arithmetic: 164 us -> none  [the longest x19 103 us: spd_solve(): factor = jnp.linalg.cholesky(matrix)]
    all_to_all x15 -> x0, starting transfers between devices: 76.2 us -> none  [the longest x8 40.7 us: copy_for_each(): lax.all_to_all(jnp.broadcast_to(value[None], (devices, *value.shape)), ax...]
    all_to_all x15 -> x0, waiting for transfers between devices: 64.7 us -> none  [the longest x8 32 us: copy_for_each(): lax.all_to_all(jnp.broadcast_to(value[None], (devices, *value.shape)), ax...]
    all_to_all x5 -> x0, blocking collectives: 60.2 us -> none  [the longest x2 22.1 us: copy_for_each(): lax.all_to_all(jnp.broadcast_to(value[None], (devices, *value.shape)), ax...]
    pallas_call x0 -> x7, Pallas kernels: none -> 43.1 us  [call(): pl.pallas_call(body, in_specs=specs, out_specs=[whole() for _ in outs], o...]
    ppermute x0 -> x19, waiting for transfers between devices: none -> 40.1 us  [turned(): lax.ppermute(value, axis, [(i, (i + by) % devices) for i in range(devices)])]
    ppermute x0 -> x19, starting transfers between devices: none -> 21.1 us  [turned(): lax.ppermute(value, axis, [(i, (i + by) % devices) for i in range(devices)])]
    another operation x37 -> x0, local copies, waits for them, and re-layouts: 13.3 us -> none  [the longest x22 12 us: spd_solve(): return jax.scipy.linalg.cho_solve((factor, True), targets)]
  transfers between devices with their start and end apart: 20 -> 24, of which waited for: 12 -> 21; matrix products, arithmetic and copies ran while one was open for 31% -> 1% of each run, Pallas kernels for 0% -> 0%
where the time goes in v1:
time: 147 us
  waiting for transfers between devices  52.1 us (35%)
  Pallas kernels  43.1 us (29%)
  starting transfers between devices  41.2 us (28%)
  local copies, waits for them, and re-layouts  6.5 us (4%)
  other arithmetic  2.27 us (2%)
    pallas_call x7, Pallas kernels, call(): pl.pallas_call(body, in_specs=specs, out_specs=[whole() for _ in outs], o...  43.1 us
    ppermute x19, waiting for transfers between devices, turned(): lax.ppermute(value, axis, [(i, (i + by) % devices) for i in range(devices)])  40.1 us
    ppermute x19, starting transfers between devices, turned(): lax.ppermute(value, axis, [(i, (i + by) % devices) for i in range(devices)])  21.1 us
    ppermute x5, starting transfers between devices, shifted(): return lax.ppermute(value, axis, pairs)  20.1 us
    ppermute x5, waiting for transfers between devices, shifted(): return lax.ppermute(value, axis, pairs)  12 us
    unnamed x40, local copies, waits for them, and re-layouts  3.44 us
  transfers between devices with their start and end apart: 24, of which 21 were waited for; matrix products, arithmetic and copies ran while one was open for 1% of the time, Pallas kernels for 0%

profile of v1, /device:TPU:1, one launch (start us, length us, event | category | flops | bytes accessed | tf_op | source)
XLA Modules:
  0.0 146.6 jit_solution(17815300935546000237)
XLA Ops:
  1.3 1.2 pad_add_fusion.sc
  2.5 1.7 %lower.1.own_ref.w_ref = bf16[272,256]{1,0:T(8,128)(2,1)} custom-call(s32[6]{0:T(128)} %pad_add_fusion.sc, f32[256,256]{1,0:T(8,128)} %bitcast.27), custom_call_target="tpu_custom_call" | custom-call | tf_op jit(solution)/shard_map/lower/pallas_call | solution.py:48
  4.2 3.6 %collective-permute-start.2 = (bf16[272,256]{1,0:T(8,128)(2,1)}, bf16[272,256]{1,0:T(8,128)(2,1)S(1)}, u32[]{:S(2)}, u32[]{:S(2)}) collective-permute-start(bf16[272,256]{1,0:T(8,128)(2,1)} %lower.1.own_ref.w_ref), channel_id=1, source_target_pairs={{0,3},{1,0},{2,1},{3,2},{4,7},{5,4},{6,5},{7,6},{8,11},{9,8},{10,9... | collective-permute-start | bytes 417800 | tf_op jit(solution)/shard_map/ppermute | solution.py:24
  7.7 2.9 %collective-permute-start.3 = (s32[512]{0:T(512)}, s32[512]{0:T(512)S(1)}, u32[]{:S(2)}, u32[]{:S(2)}) collective-permute-start(s32[512]{0:T(512)} %bitcast.31), channel_id=1, source_target_pairs={{4,0},{8,4},{12,8},{16,12},{20,16},{24,20},{28,24},{32,28},{36,32}... | collective-permute-start | bytes 6152 | tf_op jit(solution)/shard_map/ppermute | solution.py:19
  11.0 0.7 collective-permute-start
  11.7 1.9 %collective-permute-done.3 = s32[512]{0:T(512)S(1)} collective-permute-done((s32[512]{0:T(512)}, s32[512]{0:T(512)S(1)}, u32[]{:S(2)}, u32[]{:S(2)}) %collective-permute-start.3) | collective-permute-done | bytes 2080 | tf_op jit(solution)/shard_map/ppermute | solution.py:19
  13.6 0.9 copy.7.later_ref
  14.5 3.4 %collective-permute-done.1.b_ref = bf16[272,256]{1,0:T(8,128)(2,1)S(1)} collective-permute-done((bf16[272,256]{1,0:T(8,128)(2,1)}, bf16[272,256]{1,0:T(8,128)(2,1)S(1)}, u32[]{:S(2)}, u32[]{:S(2)}) %collective-permute-start.1) | collective-permute-done | bytes 139296 | tf_op jit(solution)/shard_map/ppermute | solution.py:24
  17.8 3.1 %collective-permute-done.a_ref = bf16[272,256]{1,0:T(8,128)(2,1)S(1)} collective-permute-done((bf16[272,256]{1,0:T(8,128)(2,1)}, bf16[272,256]{1,0:T(8,128)(2,1)S(1)}, u32[]{:S(2)}, u32[]{:S(2)}) %collective-permute-start) | collective-permute-done | bytes 139296 | tf_op jit(solution)/shard_map/ppermute | solution.py:24
  20.9 1.3 concatenate.8.sc
  22.3 2.6 %pick.1 = (bf16[1024,256]{1,0:T(8,128)(2,1)}, bf16[528,256]{1,0:T(8,128)(2,1)}) custom-call(s32[15]{0:T(128)} %concatenate.8.sc, bf16[272,256]{1,0:T(8,128)(2,1)} %lower.1.own_ref.w_ref, bf16[272,256]{1,0:T(8,128)(2,1)} %copy-done.12, bf16[272,256]{1,0:T(8,128)(2,1)} %copy-done.11, bf16[272,256]{1,0:T(8,128)(2,1)} %copy-done.10, s32[512,1]{1,0:T(8,128)} %copy.7.later_ref), custom_call_target="tpu_custom_call" | custom-call | tf_op jit(solution)/shard_map/pick/pallas_call | solution.py:48
  24.8 4.0 %collective-permute-start.4 = (bf16[528,256]{1,0:T(8,128)(2,1)}, bf16[528,256]{1,0:T(8,128)(2,1)S(1)}, u32[]{:S(2)}, u32[]{:S(2)}) collective-permute-start(bf16[528,256]{1,0:T(8,128)(2,1)} %get-tuple-element.17), channel_id=1, source_target_pairs={{0,4},{4,8},{8,12},{12,16},{16,20},{20,24},{24,28},{28,32},{32,36}... | collective-permute-start | bytes 811016 | tf_op jit(solution)/shard_map/ppermute | solution.py:19
  28.8 3.7 %collective-permute-done.4.halo_ref.bor_ref = bf16[528,256]{1,0:T(8,128)(2,1)S(1)} collective-permute-done((bf16[528,256]{1,0:T(8,128)(2,1)}, bf16[528,256]{1,0:T(8,128)(2,1)S(1)}, u32[]{:S(2)}, u32[]{:S(2)}) %collective-permute-start.4) | collective-permute-done | bytes 270368 | tf_op jit(solution)/shard_map/ppermute | solution.py:19
  32.5 0.7 copy-done
  33.2 2.7 %first.1.own_ref = bf16[384,256]{1,0:T(8,128)(2,1)} custom-call(bf16[384,1536]{1,0:T(8,128)(2,1)} %bitcast.25, bf16[1024,256]{1,0:T(8,128)(2,1)} %get-tuple-element.16.wg_ref, bf16[528,256]{1,0:T(8,128)(2,1)} %copy-done), custom_call_target="tpu_custom_call" | custom-call | tf_op jit(solution)/shard_map/first/pallas_call | solution.py:48
  36.5 0.8 collective-permute-start.5
  37.4 4.3 %collective-permute-done.7.c_ref = bf16[384,256]{1,0:T(8,128)(2,1)S(1)} collective-permute-done((bf16[384,256]{1,0:T(8,128)(2,1)}, bf16[384,256]{1,0:T(8,128)(2,1)S(1)}, u32[]{:S(2)}, u32[]{:S(2)}) %collective-permute-start.7) | collective-permute-done | bytes 196640 | tf_op jit(solution)/shard_map/ppermute | solution.py:24
  41.7 1.8 %collective-permute-done.6.b_ref = bf16[384,256]{1,0:T(8,128)(2,1)S(1)} collective-permute-done((bf16[384,256]{1,0:T(8,128)(2,1)}, bf16[384,256]{1,0:T(8,128)(2,1)S(1)}, u32[]{:S(2)}, u32[]{:S(2)}) %collective-permute-start.6) | collective-permute-done | bytes 196640 | tf_op jit(solution)/shard_map/ppermute | solution.py:24
  43.5 1.9 %collective-permute-done.5.a_ref = bf16[384,256]{1,0:T(8,128)(2,1)S(1)} collective-permute-done((bf16[384,256]{1,0:T(8,128)(2,1)}, bf16[384,256]{1,0:T(8,128)(2,1)S(1)}, u32[]{:S(2)}, u32[]{:S(2)}) %collective-permute-start.5) | collective-permute-done | bytes 196640 | tf_op jit(solution)/shard_map/ppermute | solution.py:24
  45.5 0.7 copy-done.9
  46.1 2.6 %spread.1 = (bf16[1536,256]{1,0:T(8,128)(2,1)}, bf16[512,256]{1,0:T(8,128)(2,1)}, bf16[512,256]{1,0:T(8,128)(2,1)}) custom-call(s32[15]{0:T(128)} %concatenate.8.sc, bf16[384,256]{1,0:T(8,128)(2,1)} %first.1.own_ref, bf16[384,256]{1,0:T(8,128)(2,1)} %copy-done.9, bf16[384,256]{1,0:T(8,128)(2,1)} %copy-done.8, bf16[384,256]{1,0:T(8,128)(2,1)} %copy-done.7, ...), custom_call_target="tpu_custom_call" | custom-call | tf_op jit(solution)/shard_map/spread/pallas_call | solution.py:48
  48.7 1.9 %collective-permute-start.8 = (bf16[512,256]{1,0:T(8,128)(2,1)}, bf16[512,256]{1,0:T(8,128)(2,1)S(1)}, u32[]{:S(2)}, u32[]{:S(2)}) collective-permute-start(bf16[512,256]{1,0:T(8,128)(2,1)} %get-tuple-element.19), channel_id=1, source_target_pairs={{4,0},{8,4},{12,8},{16,12},{20,16},{24,20},{28,24},{32,28},{36,32}... | collective-permute-start | bytes 786440 | tf_op jit(solution)/shard_map/ppermute | solution.py:19
  50.7 7.4 %collective-permute-start.9 = (bf16[512,256]{1,0:T(8,128)(2,1)}, bf16[512,256]{1,0:T(8,128)(2,1)S(1)}, u32[]{:S(2)}, u32[]{:S(2)}) collective-permute-start(bf16[512,256]{1,0:T(8,128)(2,1)} %get-tuple-element.20), channel_id=1, source_target_pairs={{0,4},{4,8},{8,12},{12,16},{16,20},{20,24},{24,28},{28,32},{32,36}... | collective-permute-start | bytes 786440 | tf_op jit(solution)/shard_map/ppermute | solution.py:19
  58.1 0.9 copy.9.map_ref
  59.0 1.4 collective-permute-done.8.ret_ref
  60.4 1.3 collective-permute-done.9.zp_ref
  61.7 0.7 copy-done.3
  62.4 4.0 %second.1 = (bf16[384,256]{1,0:T(8,128)(2,1)}, f32[1024,256]{1,0:T(8,128)}, bf16[1024,256]{1,0:T(8,128)(2,1)}, bf16[512,256]{1,0:T(8,128)(2,1)}) custom-call(s32[15]{0:T(128)} %concatenate.8.sc, bf16[384,1536]{1,0:T(8,128)(2,1)} %bitcast.26, bf16[1536,256]{1,0:T(8,128)(2,1)} %get-tuple-element.18.zg_ref, bf16[512,256]{1,0:T(8,128)(2,1)} %copy-done.2, ...), custom_call_target="tpu_custom_call" | custom-call | tf_op jit(solution)/shard_map/second/pallas_call | solution.py:48
  66.4 1.2 collective-permute-start.12
  68.3 2.8 %collective-permute-done.12.c_ref = bf16[384,256]{1,0:T(8,128)(2,1)S(1)} collective-permute-done((bf16[384,256]{1,0:T(8,128)(2,1)}, bf16[384,256]{1,0:T(8,128)(2,1)S(1)}, u32[]{:S(2)}, u32[]{:S(2)}) %collective-permute-start.12) | collective-permute-done | bytes 196640 | tf_op jit(solution)/shard_map/ppermute | solution.py:24
  71.2 2.8 %collective-permute-done.11.b_ref = bf16[384,256]{1,0:T(8,128)(2,1)S(1)} collective-permute-done((bf16[384,256]{1,0:T(8,128)(2,1)}, bf16[384,256]{1,0:T(8,128)(2,1)S(1)}, u32[]{:S(2)}, u32[]{:S(2)}) %collective-permute-start.11) | collective-permute-done | bytes 196640 | tf_op jit(solution)/shard_map/ppermute | solution.py:24
  74.0 1.7 %collective-permute-done.10.a_ref = bf16[384,256]{1,0:T(8,128)(2,1)S(1)} collective-permute-done((bf16[384,256]{1,0:T(8,128)(2,1)}, bf16[384,256]{1,0:T(8,128)(2,1)S(1)}, u32[]{:S(2)}, u32[]{:S(2)}) %collective-permute-start.10) | collective-permute-done | bytes 196640 | tf_op jit(solution)/shard_map/ppermute | solution.py:24
  76.4 3.6 %gram.1 = (f32[264,128]{1,0:T(8,128)}, bf16[256,256]{1,0:T(8,128)(2,1)}, bf16[256,256]{1,0:T(8,128)(2,1)}) custom-call(s32[15]{0:T(128)} %concatenate.8.sc, bf16[384,256]{1,0:T(8,128)(2,1)} %get-tuple-element.21.own_ref, bf16[384,256]{1,0:T(8,128)(2,1)} %copy-done.6, bf16[384,256]{1,0:T(8,128)(2,1)} %copy-done.5, bf16[384,256]{1,0:T(8,128)(2,1)} %copy-done.4, ...), custom_call_target="tpu_custom_call" | custom-call | tf_op jit(solution)/shard_map/gram/pallas_call | solution.py:48
  80.1 1.6 %collective-permute-done.13 = f32[264,128]{1,0:T(8,128)S(1)} collective-permute-done((f32[264,128]{1,0:T(8,128)}, f32[264,128]{1,0:T(8,128)S(1)}, u32[]{:S(2)}, u32[]{:S(2)}) %collective-permute-start.13) | collective-permute-done | bytes 135200 | tf_op jit(solution)/shard_map/ppermute | solution.py:24
  81.6 0.9 add.29
  82.6 7.4 %collective-permute-start.16 = (f32[264,128]{1,0:T(8,128)S(1)}, f32[264,128]{1,0:T(8,128)S(1)}, u32[]{:S(2)}, u32[]{:S(2)}) collective-permute-start(f32[264,128]{1,0:T(8,128)S(1)} %add.29), channel_id=1, source_target_pairs={{0,96},{32,0},{64,32},{96,64},{1,97},{33,1},{65,33},{97,65},{2,98}... | collective-permute-start | bytes 405512 | tf_op jit(solution)/shard_map/ppermute | solution.py:24
  91.1 4.2 %collective-permute-done.16 = f32[264,128]{1,0:T(8,128)S(1)} collective-permute-done((f32[264,128]{1,0:T(8,128)S(1)}, f32[264,128]{1,0:T(8,128)S(1)}, u32[]{:S(2)}, u32[]{:S(2)}) %collective-permute-start.16) | collective-permute-done | bytes 135200 | tf_op jit(solution)/shard_map/ppermute | solution.py:24
  95.3 0.7 collective-permute-done.15
  96.0 3.9 %collective-permute-done.14 = f32[264,128]{1,0:T(8,128)S(1)} collective-permute-done((f32[264,128]{1,0:T(8,128)S(1)}, f32[264,128]{1,0:T(8,128)S(1)}, u32[]{:S(2)}, u32[]{:S(2)}) %collective-permute-start.14) | collective-permute-done | bytes 135200 | tf_op jit(solution)/shard_map/ppermute | solution.py:24
  100.0 2.8 %collective-permute-start.18 = (f32[264,128]{1,0:T(8,128)S(1)}, f32[264,128]{1,0:T(8,128)S(1)}, u32[]{:S(2)}, u32[]{:S(2)}) collective-permute-start(f32[264,128]{1,0:T(8,128)S(1)} %add_add_fusion.1), channel_id=1, source_target_pairs={{0,16},{8,24},{16,0},{24,8},{1,17},{9,25},{17,1},{25,9},{2,18},{10... | collective-permute-start | bytes 405512 | tf_op jit(solution)/shard_map/ppermute | solution.py:24
  102.8 1.8 %collective-permute-done.19 = f32[264,128]{1,0:T(8,128)S(1)} collective-permute-done((f32[264,128]{1,0:T(8,128)S(1)}, f32[264,128]{1,0:T(8,128)S(1)}, u32[]{:S(2)}, u32[]{:S(2)}) %collective-permute-start.19) | collective-permute-done | bytes 135200 | tf_op jit(solution)/shard_map/ppermute | solution.py:24
  104.6 1.2 collective-permute-done.18
  105.9 3.7 %collective-permute-done.17 = f32[264,128]{1,0:T(8,128)S(1)} collective-permute-done((f32[264,128]{1,0:T(8,128)S(1)}, f32[264,128]{1,0:T(8,128)S(1)}, u32[]{:S(2)}, u32[]{:S(2)}) %collective-permute-start.17) | collective-permute-done | bytes 135200 | tf_op jit(solution)/shard_map/ppermute | solution.py:24
  109.6 1.0 collective-permute-start.22
  111.2 3.9 %collective-permute-start.23 = (bf16[256,256]{1,0:T(8,128)(2,1)S(1)}, bf16[256,256]{1,0:T(8,128)(2,1)S(1)}, u32[]{:S(2)}, u32[]{:S(2)}) collective-permute-start(bf16[256,256]{1,0:T(8,128)(2,1)S(1)} %copy-done.19), channel_id=1, source_target_pairs={{4,0},{8,4},{12,8},{16,12},{20,16},{24,20},{28,24},{32,28},{36,32}... | collective-permute-start | bytes 393224 | tf_op jit(solution)/shard_map/ppermute | solution.py:19
  115.1 3.7 %collective-permute-done.23.ret_ref = bf16[256,256]{1,0:T(8,128)(2,1)S(1)} collective-permute-done((bf16[256,256]{1,0:T(8,128)(2,1)S(1)}, bf16[256,256]{1,0:T(8,128)(2,1)S(1)}, u32[]{:S(2)}, u32[]{:S(2)}) %collective-permute-start.23) | collective-permute-done | bytes 131104 | tf_op jit(solution)/shard_map/ppermute | solution.py:19
  118.8 1.2 collective-permute-done.20.a_ref
  120.7 26.0 %solve.1 = (f32[256,256]{1,0:T(8,128)}, f32[256,256]{1,0:T(8,128)}) custom-call(s32[15]{0:T(128)} %concatenate.8.sc, f32[264,128]{1,0:T(8,128)} %copy-done.1, f32[264,128]{1,0:T(8,128)} %copy-done.15, f32[264,128]{1,0:T(8,128)} %copy-done.14, f32[264,128]{1,0:T(8,128)} %copy-done.13, f32[256,256]{1,0:T(8,128)} %bitcast.28, ...), custom_call_target="tpu_custom_call" | custom-call | tf_op jit(solution)/shard_map/solve/pallas_call | solution.py:48
  (57 shorter events, 5.1 us)
Async XLA Ops:
  4.2 10.3 %collective-permute-start.2 = (bf16[272,256]{1,0:T(8,128)(2,1)}, bf16[272,256]{1,0:T(8,128)(2,1)S(1)}, u32[]{:S(2)}, u32[]{:S(2)}) collective-permute-start(bf16[272,256]{1,0:T(8,128)(2,1)} %lower.1.own_ref.w_ref), channel_id=1, source_target_pairs={{0,3},{1,0},{2,1},{3,2},{4,7},{5,4},{6,5},{7,6},{8,11},{9,8},{10,9... | collective-permute-start | bytes 417800 | tf_op jit(solution)/shard_map/ppermute | solution.py:24
  7.7 5.8 %collective-permute-start.3 = (s32[512]{0:T(512)}, s32[512]{0:T(512)S(1)}, u32[]{:S(2)}, u32[]{:S(2)}) collective-permute-start(s32[512]{0:T(512)} %bitcast.31), channel_id=1, source_target_pairs={{4,0},{8,4},{12,8},{16,12},{20,16},{24,20},{28,24},{32,28},{36,32}... | collective-permute-start | bytes 6152 | tf_op jit(solution)/shard_map/ppermute | solution.py:19
  10.6 7.2 %collective-permute-start.1 = (bf16[272,256]{1,0:T(8,128)(2,1)}, bf16[272,256]{1,0:T(8,128)(2,1)S(1)}, u32[]{:S(2)}, u32[]{:S(2)}) collective-permute-start(bf16[272,256]{1,0:T(8,128)(2,1)} %lower.1.own_ref.w_ref), channel_id=1, source_target_pairs={{0,2},{1,3},{2,0},{3,1},{4,6},{5,7},{6,4},{7,5},{8,10},{9,11},{10,... | collective-permute-start | bytes 417800 | tf_op jit(solution)/shard_map/ppermute | solution.py:24
  11.0 9.9 %collective-permute-start = (bf16[272,256]{1,0:T(8,128)(2,1)}, bf16[272,256]{1,0:T(8,128)(2,1)S(1)}, u32[]{:S(2)}, u32[]{:S(2)}) collective-permute-start(bf16[272,256]{1,0:T(8,128)(2,1)} %lower.1.own_ref.w_ref), channel_id=1, source_target_pairs={{0,1},{1,2},{2,3},{3,0},{4,5},{5,6},{6,7},{7,4},{8,9},{9,10},{10,1... | collective-permute-start | bytes 417800 | tf_op jit(solution)/shard_map/ppermute | solution.py:24
  13.6 22.3 %copy-start.17 = (s32[512]{0:T(512)}, s32[512]{0:T(512)S(1)}, u32[]{:S(2)}) copy-start(s32[512]{0:T(512)S(1)} %collective-permute-done.3) | copy-start | bytes 6148
  14.5 7.8 %copy-start.10 = (bf16[272,256]{1,0:T(8,128)(2,1)}, bf16[272,256]{1,0:T(8,128)(2,1)S(1)}, u32[]{:S(2)}) copy-start(bf16[272,256]{1,0:T(8,128)(2,1)S(1)} %collective-permute-done.2.c_ref) | copy-start | bytes 417796
  17.8 4.4 %copy-start.11 = (bf16[272,256]{1,0:T(8,128)(2,1)}, bf16[272,256]{1,0:T(8,128)(2,1)S(1)}, u32[]{:S(2)}) copy-start(bf16[272,256]{1,0:T(8,128)(2,1)S(1)} %collective-permute-done.1.b_ref) | copy-start | bytes 417796
  20.9 1.4 copy-start.12
  24.8 7.7 %collective-permute-start.4 = (bf16[528,256]{1,0:T(8,128)(2,1)}, bf16[528,256]{1,0:T(8,128)(2,1)S(1)}, u32[]{:S(2)}, u32[]{:S(2)}) collective-permute-start(bf16[528,256]{1,0:T(8,128)(2,1)} %get-tuple-element.17), channel_id=1, source_target_pairs={{0,4},{4,8},{8,12},{12,16},{16,20},{20,24},{24,28},{28,32},{32,36}... | collective-permute-start | bytes 811016 | tf_op jit(solution)/shard_map/ppermute | solution.py:19
  32.5 0.7 copy-start
  33.2 24.9 %copy-start.18 = (s32[1,512]{1,0:T(1,128)S(1)}, s32[1,512]{1,0:T(1,128)}, u32[]{:S(2)}) copy-start(s32[1,512]{1,0:T(1,128)} %map_ref.1) | copy-start | bytes 6148
  35.9 5.8 %collective-permute-start.7 = (bf16[384,256]{1,0:T(8,128)(2,1)}, bf16[384,256]{1,0:T(8,128)(2,1)S(1)}, u32[]{:S(2)}, u32[]{:S(2)}) collective-permute-start(bf16[384,256]{1,0:T(8,128)(2,1)} %first.1.own_ref), channel_id=1, source_target_pairs={{0,3},{1,0},{2,1},{3,2},{4,7},{5,4},{6,5},{7,6},{8,11},{9,8},{10,9... | collective-permute-start | bytes 589832 | tf_op jit(solution)/shard_map/ppermute | solution.py:24
  36.2 7.3 %collective-permute-start.6 = (bf16[384,256]{1,0:T(8,128)(2,1)}, bf16[384,256]{1,0:T(8,128)(2,1)S(1)}, u32[]{:S(2)}, u32[]{:S(2)}) collective-permute-start(bf16[384,256]{1,0:T(8,128)(2,1)} %first.1.own_ref), channel_id=1, source_target_pairs={{0,2},{1,3},{2,0},{3,1},{4,6},{5,7},{6,4},{7,5},{8,10},{9,11},{10,... | collective-permute-start | bytes 589832 | tf_op jit(solution)/shard_map/ppermute | solution.py:24
  36.5 8.9 %collective-permute-start.5 = (bf16[384,256]{1,0:T(8,128)(2,1)}, bf16[384,256]{1,0:T(8,128)(2,1)S(1)}, u32[]{:S(2)}, u32[]{:S(2)}) collective-permute-start(bf16[384,256]{1,0:T(8,128)(2,1)} %first.1.own_ref), channel_id=1, source_target_pairs={{0,1},{1,2},{2,3},{3,0},{4,5},{5,6},{6,7},{7,4},{8,9},{9,10},{10,1... | collective-permute-start | bytes 589832 | tf_op jit(solution)/shard_map/ppermute | solution.py:24
  41.7 3.8 %copy-start.7 = (bf16[384,256]{1,0:T(8,128)(2,1)}, bf16[384,256]{1,0:T(8,128)(2,1)S(1)}, u32[]{:S(2)}) copy-start(bf16[384,256]{1,0:T(8,128)(2,1)S(1)} %collective-permute-done.7.c_ref) | copy-start | bytes 589828
  43.5 1.9 %copy-start.8 = (bf16[384,256]{1,0:T(8,128)(2,1)}, bf16[384,256]{1,0:T(8,128)(2,1)S(1)}, u32[]{:S(2)}) copy-start(bf16[384,256]{1,0:T(8,128)(2,1)S(1)} %collective-permute-done.6.b_ref) | copy-start | bytes 589828
  45.5 0.7 copy-start.9
  48.7 11.7 %collective-permute-start.8 = (bf16[512,256]{1,0:T(8,128)(2,1)}, bf16[512,256]{1,0:T(8,128)(2,1)S(1)}, u32[]{:S(2)}, u32[]{:S(2)}) collective-permute-start(bf16[512,256]{1,0:T(8,128)(2,1)} %get-tuple-element.19), channel_id=1, source_target_pairs={{4,0},{8,4},{12,8},{16,12},{20,16},{24,20},{28,24},{32,28},{36,32}... | collective-permute-start | bytes 786440 | tf_op jit(solution)/shard_map/ppermute | solution.py:19
  50.7 11.1 %collective-permute-start.9 = (bf16[512,256]{1,0:T(8,128)(2,1)}, bf16[512,256]{1,0:T(8,128)(2,1)S(1)}, u32[]{:S(2)}, u32[]{:S(2)}) collective-permute-start(bf16[512,256]{1,0:T(8,128)(2,1)} %get-tuple-element.20), channel_id=1, source_target_pairs={{0,4},{4,8},{8,12},{12,16},{16,20},{20,24},{24,28},{28,32},{32,36}... | collective-permute-start | bytes 786440 | tf_op jit(solution)/shard_map/ppermute | solution.py:19
  60.4 1.3 copy-start.2
  61.7 0.7 copy-start.3
  66.4 4.7 %collective-permute-start.12 = (bf16[384,256]{1,0:T(8,128)(2,1)}, bf16[384,256]{1,0:T(8,128)(2,1)S(1)}, u32[]{:S(2)}, u32[]{:S(2)}) collective-permute-start(bf16[384,256]{1,0:T(8,128)(2,1)} %get-tuple-element.21.own_ref), channel_id=1, source_target_pairs={{0,3},{1,0},{2,1},{3,2},{4,7},{5,4},{6,5},{7,6},{8,11},{9,8},{10,9... | collective-permute-start | bytes 589832 | tf_op jit(solution)/shard_map/ppermute | solution.py:24
  67.7 6.3 %collective-permute-start.11 = (bf16[384,256]{1,0:T(8,128)(2,1)}, bf16[384,256]{1,0:T(8,128)(2,1)S(1)}, u32[]{:S(2)}, u32[]{:S(2)}) collective-permute-start(bf16[384,256]{1,0:T(8,128)(2,1)} %get-tuple-element.21.own_ref), channel_id=1, source_target_pairs={{0,2},{1,3},{2,0},{3,1},{4,6},{5,7},{6,4},{7,5},{8,10},{9,11},{10,... | collective-permute-start | bytes 589832 | tf_op jit(solution)/shard_map/ppermute | solution.py:24
  67.7 8.1 %collective-permute-start.10 = (bf16[384,256]{1,0:T(8,128)(2,1)}, bf16[384,256]{1,0:T(8,128)(2,1)S(1)}, u32[]{:S(2)}, u32[]{:S(2)}) collective-permute-start(bf16[384,256]{1,0:T(8,128)(2,1)} %get-tuple-element.21.own_ref), channel_id=1, source_target_pairs={{0,1},{1,2},{2,3},{3,0},{4,5},{5,6},{6,7},{7,4},{8,9},{9,10},{10,1... | collective-permute-start | bytes 589832 | tf_op jit(solution)/shard_map/ppermute | solution.py:24
  71.2 4.6 %copy-start.4 = (bf16[384,256]{1,0:T(8,128)(2,1)}, bf16[384,256]{1,0:T(8,128)(2,1)S(1)}, u32[]{:S(2)}) copy-start(bf16[384,256]{1,0:T(8,128)(2,1)S(1)} %collective-permute-done.12.c_ref) | copy-start | bytes 589828
  74.0 1.7 %copy-start.5 = (bf16[384,256]{1,0:T(8,128)(2,1)}, bf16[384,256]{1,0:T(8,128)(2,1)S(1)}, u32[]{:S(2)}) copy-start(bf16[384,256]{1,0:T(8,128)(2,1)S(1)} %collective-permute-done.11.b_ref) | copy-start | bytes 589828
  75.8 0.7 copy-start.6
  80.1 31.1 %copy-start.19 = (bf16[256,256]{1,0:T(8,128)(2,1)S(1)}, bf16[256,256]{1,0:T(8,128)(2,1)}, u32[]{:S(2)}) copy-start(bf16[256,256]{1,0:T(8,128)(2,1)} %get-tuple-element.27) | copy-start | bytes 393220
  80.1 1.6 %collective-permute-start.13 = (f32[264,128]{1,0:T(8,128)}, f32[264,128]{1,0:T(8,128)S(1)}, u32[]{:S(2)}, u32[]{:S(2)}) collective-permute-start(f32[264,128]{1,0:T(8,128)} %get-tuple-element.25), channel_id=1, source_target_pairs={{0,4},{4,0},{1,5},{5,1},{2,6},{6,2},{3,7},{7,3},{8,12},{12,8},{9,1... | collective-permute-start | bytes 405512 | tf_op jit(solution)/shard_map/ppermute | solution.py:24
  82.6 12.7 %collective-permute-start.16 = (f32[264,128]{1,0:T(8,128)S(1)}, f32[264,128]{1,0:T(8,128)S(1)}, u32[]{:S(2)}, u32[]{:S(2)}) collective-permute-start(f32[264,128]{1,0:T(8,128)S(1)} %add.29), channel_id=1, source_target_pairs={{0,96},{32,0},{64,32},{96,64},{1,97},{33,1},{65,33},{97,65},{2,98}... | collective-permute-start | bytes 405512 | tf_op jit(solution)/shard_map/ppermute | solution.py:24
  90.0 6.0 %collective-permute-start.15 = (f32[264,128]{1,0:T(8,128)S(1)}, f32[264,128]{1,0:T(8,128)S(1)}, u32[]{:S(2)}, u32[]{:S(2)}) collective-permute-start(f32[264,128]{1,0:T(8,128)S(1)} %add.29), channel_id=1, source_target_pairs={{0,64},{32,96},{64,0},{96,32},{1,65},{33,97},{65,1},{97,33},{2,66}... | collective-permute-start | bytes 405512 | tf_op jit(solution)/shard_map/ppermute | solution.py:24
  90.5 9.4 %collective-permute-start.14 = (f32[264,128]{1,0:T(8,128)S(1)}, f32[264,128]{1,0:T(8,128)S(1)}, u32[]{:S(2)}, u32[]{:S(2)}) collective-permute-start(f32[264,128]{1,0:T(8,128)S(1)} %add.29), channel_id=1, source_target_pairs={{0,32},{32,64},{64,96},{96,0},{1,33},{33,65},{65,97},{97,1},{2,34}... | collective-permute-start | bytes 405512 | tf_op jit(solution)/shard_map/ppermute | solution.py:24
  99.9 4.7 %collective-permute-start.19 = (f32[264,128]{1,0:T(8,128)S(1)}, f32[264,128]{1,0:T(8,128)S(1)}, u32[]{:S(2)}, u32[]{:S(2)}) collective-permute-start(f32[264,128]{1,0:T(8,128)S(1)} %add_add_fusion.1), channel_id=1, source_target_pairs={{0,24},{8,0},{16,8},{24,16},{1,25},{9,1},{17,9},{25,17},{2,26},{10... | collective-permute-start | bytes 405512 | tf_op jit(solution)/shard_map/ppermute | solution.py:24
  100.0 5.8 %collective-permute-start.18 = (f32[264,128]{1,0:T(8,128)S(1)}, f32[264,128]{1,0:T(8,128)S(1)}, u32[]{:S(2)}, u32[]{:S(2)}) collective-permute-start(f32[264,128]{1,0:T(8,128)S(1)} %add_add_fusion.1), channel_id=1, source_target_pairs={{0,16},{8,24},{16,0},{24,8},{1,17},{9,25},{17,1},{25,9},{2,18},{10... | collective-permute-start | bytes 405512 | tf_op jit(solution)/shard_map/ppermute | solution.py:24
  102.8 6.7 %collective-permute-start.17 = (f32[264,128]{1,0:T(8,128)S(1)}, f32[264,128]{1,0:T(8,128)S(1)}, u32[]{:S(2)}, u32[]{:S(2)}) collective-permute-start(f32[264,128]{1,0:T(8,128)S(1)} %add_add_fusion.1), channel_id=1, source_target_pairs={{0,8},{8,16},{16,24},{24,0},{1,9},{9,17},{17,25},{25,1},{2,10},{10... | collective-permute-start | bytes 405512 | tf_op jit(solution)/shard_map/ppermute | solution.py:24
  109.5 10.5 %copy-start.1 = (f32[264,128]{1,0:T(8,128)}, f32[264,128]{1,0:T(8,128)S(1)}, u32[]{:S(2)}) copy-start(f32[264,128]{1,0:T(8,128)S(1)} %add_add_fusion.own_ref) | copy-start | bytes 405508
  109.6 9.2 %collective-permute-start.22 = (f32[264,128]{1,0:T(8,128)S(1)}, f32[264,128]{1,0:T(8,128)S(1)}, u32[]{:S(2)}, u32[]{:S(2)}) collective-permute-start(f32[264,128]{1,0:T(8,128)S(1)} %add_add_fusion.own_ref), channel_id=1, source_target_pairs={{0,3},{1,0},{2,1},{3,2},{4,7},{5,4},{6,5},{7,6},{8,11},{9,8},{10,9... | collective-permute-start | bytes 405512 | tf_op jit(solution)/shard_map/ppermute | solution.py:24
  110.5 8.3 %collective-permute-start.21 = (f32[264,128]{1,0:T(8,128)S(1)}, f32[264,128]{1,0:T(8,128)S(1)}, u32[]{:S(2)}, u32[]{:S(2)}) collective-permute-start(f32[264,128]{1,0:T(8,128)S(1)} %add_add_fusion.own_ref), channel_id=1, source_target_pairs={{0,2},{1,3},{2,0},{3,1},{4,6},{5,7},{6,4},{7,5},{8,10},{9,11},{10,... | collective-permute-start | bytes 405512 | tf_op jit(solution)/shard_map/ppermute | solution.py:24
  110.7 9.3 %collective-permute-start.20 = (f32[264,128]{1,0:T(8,128)S(1)}, f32[264,128]{1,0:T(8,128)S(1)}, u32[]{:S(2)}, u32[]{:S(2)}) collective-permute-start(f32[264,128]{1,0:T(8,128)S(1)} %add_add_fusion.own_ref), channel_id=1, source_target_pairs={{0,1},{1,2},{2,3},{3,0},{4,5},{5,6},{6,7},{7,4},{8,9},{9,10},{10,1... | collective-permute-start | bytes 405512 | tf_op jit(solution)/shard_map/ppermute | solution.py:24
  111.2 7.6 %collective-permute-start.23 = (bf16[256,256]{1,0:T(8,128)(2,1)S(1)}, bf16[256,256]{1,0:T(8,128)(2,1)S(1)}, u32[]{:S(2)}, u32[]{:S(2)}) collective-permute-start(bf16[256,256]{1,0:T(8,128)(2,1)S(1)} %copy-done.19), channel_id=1, source_target_pairs={{4,0},{8,4},{12,8},{16,12},{20,16},{24,20},{28,24},{32,28},{36,32}... | collective-permute-start | bytes 393224 | tf_op jit(solution)/shard_map/ppermute | solution.py:19
  118.8 1.2 copy-start.16
  118.8 1.2 copy-start.13
  118.8 1.2 copy-start.14
  120.0 0.7 copy-start.15

commit v2 on v1

v2 whole, which is shorter than its diff:
```python
import jax
import jax.numpy as jnp
from jax import lax
from jax.experimental import pallas as pl
from jax.experimental.pallas import tpu as pltpu
from jax.sharding import Mesh
from jax.sharding import PartitionSpec as P

SUB = ("sub_0", "sub_1", "sub_2")
SUB_HELP = ("sub_0", "sub_1", "sub_2", "help")
SHIFT = 3.0
BF = jnp.bfloat16
F32 = jnp.float32


def shifted(value, axis, by):
    devices = lax.axis_size(axis)
    pairs = [(i, i + by) for i in range(devices) if 0 <= i + by < devices]
    return lax.ppermute(value, axis, pairs)


def turned(value, axis, by):
    devices = lax.axis_size(axis)
    return lax.ppermute(value, axis, [(i, (i + by) % devices) for i in range(devices)])


def from_others(value, axis):
    return [turned(value, axis, by) for by in range(1, lax.axis_size(axis))]


def summed(value, axis):
    total = value
    for other in from_others(value, axis):
        total = total + other
    return total


def whole(space=None):
    return pl.BlockSpec(memory_space=pltpu.MemorySpace.VMEM if space is None else space)


def scalars():
    return pl.BlockSpec(memory_space=pltpu.MemorySpace.SMEM)


def call(body, args, outs, scratch=(), small=1, name=None):
    specs = [scalars()] * small + [whole()] * (len(args) - small)
    return pl.pallas_call(
        body,
        in_specs=specs,
        out_specs=[whole() for _ in outs],
        out_shape=[jax.ShapeDtypeStruct(s, d) for s, d in outs],
        scratch_shapes=list(scratch),
        compiler_params=pltpu.CompilerParams(vmem_limit_bytes=16 << 20),
        name=name,
    )(*args)


def iota(shape, dim):
    return lax.broadcasted_iota(jnp.int32, shape, dim)


def mm(a, b):
    return lax.dot_general(a, b, (((1,), (0,)), ((), ())), preferred_element_type=F32)


def tmm(a, b):
    return lax.dot_general(a, b, (((0,), (0,)), ((), ())), preferred_element_type=F32)


def halves(a):
    high = a.astype(BF)
    return high, (a - high.astype(F32)).astype(BF)


def mm3(a, b):
    ah, al = halves(a)
    bh, bl = halves(b)
    return mm(ah, bh) + (mm(ah, bl) + mm(al, bh))


def mmf(a, b):
    return jnp.dot(a, b, precision=lax.Precision.HIGHEST, preferred_element_type=F32)


def hot(mask):
    return jnp.where(mask, 1.0, 0.0).astype(BF)


def here():
    return lax.axis_index("help")


def lower_body(count, index, r_ref, out_ref):
    rows = r_ref.shape[0]
    cols = r_ref.shape[1]
    row = iota((rows, 1), 0) + here() * rows
    out_ref[:rows, :] = jnp.where(row < count[0], r_ref[...], 0.0).astype(BF)
    col = iota((16, cols), 1)
    info = jnp.zeros((16, cols), F32)
    values = [index[0], index[1], index[2], count[0] // 32, count[0] % 32]
    for k, value in enumerate(values):
        info = jnp.where(col == k, value.astype(F32), info)
    out_ref[rows:, :] = info.astype(BF)


def pick_body(own_ref, a_ref, b_ref, c_ref, later_ref, wg_ref, pick_ref):
    rows = own_ref.shape[0] - 16
    h = here()
    for k, ref in enumerate((own_ref, a_ref, b_ref, c_ref)):
        at = pl.multiple_of(lax.rem(h + 4 - k, 4) * rows, rows)
        wg_ref[pl.ds(at, rows), :] = ref[:rows, :]
    halo = later_ref.shape[0]
    choose = hot(later_ref[...] == iota((halo, wg_ref.shape[0]), 1))
    pick_ref[:halo, :] = mm(choose, wg_ref[...]).astype(BF)
    pick_ref[halo:, :] = own_ref[rows:, :]


def early_body(f_ref, wg_ref, z_ref):
    z_ref[...] = mm(f_ref[:, : wg_ref.shape[0]], wg_ref[...])


def first_body(f_ref, early_ref, halo_ref, z_ref):
    halo = halo_ref.shape[0] - 16
    owned = f_ref.shape[1] - halo
    z_ref[...] = (early_ref[...] - mm(f_ref[:, owned:], halo_ref[:halo, :])).astype(BF)


def spread_body(count, index, own_ref, a_ref, b_ref, c_ref, later_ref, zg_ref, halo_ref, pick_ref):
    panel = own_ref.shape[0] // 3
    for k, ref in enumerate((own_ref, a_ref, b_ref, c_ref)):
        for j in range(3):
            at = pl.multiple_of(index[3 * k + j] * panel, panel)
            zg_ref[pl.ds(at, panel), :] = ref[j * panel : (j + 1) * panel, :]
    halo = halo_ref.shape[0]
    owned = zg_ref.shape[0] - halo
    halo_ref[...] = zg_ref[owned:, :]
    later = later_ref[...]
    choose = hot((later == iota((halo, owned), 1)) & (later < count[0]))
    pick_ref[...] = mm(choose, zg_ref[:owned, :]).astype(BF)


def second_body(
    count, f_ref, zg_ref, ret_ref, zp_ref, bor_ref, wg_ref, map_ref, later_ref, z_ref, im_ref, vb_ref, vh_ref
):
    owned = wg_ref.shape[0]
    halo = ret_ref.shape[0]
    live = iota((owned, 1), 0) < count[0]
    back = mm(hot(iota((owned, halo), 0) == later_ref[...]), ret_ref[...])
    image = jnp.where(live, zg_ref[:owned, :].astype(F32) - back, 0.0)
    im_ref[...] = image
    vb = (image - SHIFT * wg_ref[...].astype(F32)).astype(BF)
    vb_ref[...] = vb
    info = bor_ref[halo : halo + 1, :].astype(F32)
    lane = iota(info.shape, 1)
    weight = jnp.where(lane == 3, 32.0, jnp.where(lane == 4, 1.0, 0.0))
    before = jnp.sum(info * weight, axis=1, keepdims=True)
    alive = (map_ref[...].astype(F32) < before) & (lax.axis_index(SUB) > 0)
    term = zp_ref[...].astype(F32) - zg_ref[owned:, :].astype(F32)
    vh = jnp.where(alive, term, 0.0) - SHIFT * bor_ref[:halo, :].astype(F32)
    vh = vh.astype(BF)
    vh_ref[...] = vh
    z = mm(f_ref[:, :owned], vb) - mm(f_ref[:, owned:], vh)
    z_ref[...] = z.astype(BF)


def gram_body(
    index, own_ref, a_ref, b_ref, c_ref, wg_ref, bor_ref, zg_ref, im_ref, vb_ref, vh_ref,
    keep_ref, give_ref, z2_ref, gram_ref, pack_ref,
):
    panel = own_ref.shape[0] // 3
    for k, ref in enumerate((own_ref, a_ref, b_ref, c_ref)):
        for j in range(3):
            at = pl.multiple_of(index[3 * k + j] * panel, panel)
            z2_ref[pl.ds(at, panel), :] = ref[j * panel : (j + 1) * panel, :]
    owned = wg_ref.shape[0]
    halo = vh_ref.shape[0]
    h = here()

    @pl.when(h == 0)
    def _():
        gram_ref[...] = tmm(wg_ref[...], wg_ref[...])

    @pl.when(h == 1)
    def _():
        gram_ref[...] = tmm(wg_ref[...], zg_ref[:owned, :]) - tmm(bor_ref[:halo, :], zg_ref[owned:, :])

    @pl.when(h == 2)
    def _():
        high, low = halves(im_ref[...])
        cross = tmm(low, high)
        gram_ref[...] = tmm(high, high) + (cross + cross.T)

    @pl.when(h == 3)
    def _():
        gram_ref[...] = tmm(vb_ref[...], z2_ref[:owned, :]) - tmm(vh_ref[...], z2_ref[owned:, :])

    half = gram_ref.shape[0] // 2
    lower = gram_ref[:half, :half]
    upper = gram_ref[half:, half:]
    r, c = iota((half, half), 0), iota((half, half), 1)
    diagonal = jnp.sum(jnp.where(r == c, upper, 0.0), axis=0, keepdims=True)
    pack_ref[0, :half, :] = jnp.where(r >= c, lower, upper.T)
    pack_ref[1, :half, :] = gram_ref[half:, :half]
    pack_ref[0, half:, :] = jnp.broadcast_to(diagonal, (8, half))
    pack_ref[1, half:, :] = jnp.zeros((8, half), F32)
    core = lax.axis_index("sub_2")
    keep_ref[...] = pack_ref[core]
    give_ref[...] = pack_ref[1 - core]


def tail_body(z_ref, map_ref, mine_ref, back_ref):
    rows = mine_ref.shape[0]
    halo = map_ref.shape[1]
    at = pl.multiple_of(here() * rows, rows)
    mine_ref[...] = z_ref[pl.ds(at, rows), :]
    choose = hot(iota((rows, halo), 0) + at == map_ref[...])
    back_ref[...] = mm(choose, z_ref[z_ref.shape[0] - halo :, :]).astype(BF)


def unpacked(pack, out_ref):
    half = pack.shape[2]
    r, c = iota((half, half), 0), iota((half, half), 1)
    both = pack[0, :half, :]
    flip = both.T
    side = pack[1, :half, :]
    out_ref[:half, :half] = jnp.where(r >= c, both, flip)
    out_ref[half:, half:] = jnp.where(r == c, pack[0, half : half + 1, :], jnp.where(r < c, both, flip))
    out_ref[half:, :half] = side
    out_ref[:half, half:] = side.T


def inverse(k, x_ref):
    n = k.shape[0]
    r, c = iota((n, n), 0), iota((n, n), 1)
    eye = jnp.where(r == c, 1.0, 0.0)
    on = jnp.where(r == c, k, 0.0)
    by_row = lax.rsqrt(jnp.sum(on, axis=1, keepdims=True))
    by_col = lax.rsqrt(jnp.sum(on, axis=0, keepdims=True))
    unit = k * by_row * by_col
    norm = jnp.max(jnp.sum(jnp.abs(unit), axis=0, keepdims=True), axis=1, keepdims=True)
    step = 2.0 / (1.0 + norm)
    high, low = halves(unit)
    x = 2.0 * eye - unit
    left = eye - mm(high, x.astype(BF))
    for _ in range(2):
        x = x + mm(x.astype(BF), left.astype(BF))
        xh, xl = halves(x)
        left = eye - (mm(high, xh) + (mm(high, xl) + mm(low, xh)))
    x_ref[...] = x + mm(x.astype(BF), left.astype(BF))

    def size(error):
        return jnp.max(jnp.sum(jnp.abs(error), axis=0, keepdims=True))

    @pl.when(jnp.logical_not(size(left) < 3e-3))
    def _():
        x_ref[...] = step * eye

        def more(state):
            return (state[0] < 60) & (state[1] > 1e-3)

        def improve(state):
            x = x_ref[...]
            left = eye - mmf(unit, x)
            x_ref[...] = x + mmf(x, left)
            return state[0] + 1, size(left)

        lax.while_loop(more, improve, (jnp.int32(0), jnp.float32(1.0)))

    return x_ref[...] * by_row * by_col


def solve_body(
    count, own_ref, a_ref, b_ref, c_ref, r_ref, im_ref, w_ref, mine_ref, ret_ref,
    sol_ref, res_ref, pack_ref, g00_ref, g01_ref, g11_ref, gvv_ref, x_ref,
):
    h = here()
    core = lax.axis_index("sub_2")
    for k, ref in enumerate((own_ref, a_ref, b_ref, c_ref)):
        at = lax.rem(h + 4 - k, 4)
        pack_ref[at, core] = ref[0]
        pack_ref[at, 1 - core] = ref[1]
    for k, ref in enumerate((g00_ref, g01_ref, g11_ref, gvv_ref)):
        unpacked(pack_ref.at[k], ref)
    g01 = g01_ref[...]
    mixed = g11_ref[...] - SHIFT * g01
    inv = inverse(g01, x_ref)
    p1 = mm3(inv, mixed)
    p2 = mm3(inv, g00_ref[...])
    schur = gvv_ref[...] - mm3(mixed, p1)
    schur = 0.5 * (schur + schur.T)
    rest = g01 - SHIFT * g00_ref[...] - mm3(mixed, p2)
    cv = mm3(inverse(schur, x_ref), rest)
    cr = p2 - mm3(p1, cv)
    rows = r_ref.shape[0]
    live = iota((rows, 1), 0) + h * rows < count[0]
    r = jnp.where(live, r_ref[...], 0.0)
    at = pl.multiple_of(h * rows, rows)
    im = im_ref[pl.ds(at, rows), :]
    v = im - SHIFT * w_ref[:rows, :].astype(F32)
    av = jnp.where(live, mine_ref[...].astype(F32) - ret_ref[...].astype(F32), 0.0)
    sol_ref[...] = mm3(r, cr) + mm3(v, cv)
    res_ref[...] = r - mm3(im, cr) - mm3(av, cv)


def shards(right_side, operator_panels, panel_index, halo_map, counts):
    rows, cols = right_side.shape[1:]
    slots, panel, wide = operator_panels.shape
    halo = halo_map.shape[1]
    half = cols // 2
    owned = rows * lax.axis_size("help")
    r = right_side.reshape(rows, cols)
    f = operator_panels.reshape(slots * panel, wide)
    later = shifted(halo_map.reshape(halo), SUB, -1)
    later_col, later_row = later.reshape(halo, 1), later.reshape(1, halo)
    map_col, map_row = halo_map.reshape(halo, 1), halo_map.reshape(1, halo)

    (low,) = call(lower_body, (counts, panel_index, r), [((rows + 16, cols), BF)], small=2, name="lower")
    others = from_others(low, "help")
    wg, pick = call(
        pick_body,
        (low, *others, later_col),
        [((owned, cols), BF), ((halo + 16, cols), BF)],
        small=0,
        name="pick",
    )
    bor = shifted(pick, SUB, 1)
    (early,) = call(early_body, (f, wg), [((slots * panel, cols), F32)], small=0, name="early")
    index = jnp.concatenate([panel_index, *(o[rows, :slots].astype(jnp.int32) for o in others)])
    (z,) = call(first_body, (f, early, bor), [((slots * panel, cols), BF)], small=0, name="first")
    zs = from_others(z, "help")
    zg, zh, zpick = call(
        spread_body,
        (counts, index, z, *zs, later_col),
        [((wide, cols), BF), ((halo, cols), BF), ((halo, cols), BF)],
        small=2,
        name="spread",
    )
    ret = shifted(zh, SUB, -1)
    zp = shifted(zpick, SUB, 1)
    z2, im, vb, vh = call(
        second_body,
        (counts, f, zg, ret, zp, bor, wg, map_col, later_row),
        [((slots * panel, cols), BF), ((owned, cols), F32), ((owned, cols), BF), ((halo, cols), BF)],
        name="second",
    )
    z2s = from_others(z2, "help")
    keep, give, z2g = call(
        gram_body,
        (index, z2, *z2s, wg, bor, zg, im, vb, vh),
        [((half + 8, half), F32), ((half + 8, half), F32), ((wide, cols), BF)],
        scratch=[pltpu.VMEM((cols, cols), F32), pltpu.VMEM((2, half + 8, half), F32)],
        name="gram",
    )
    pack = keep + turned(give, "sub_2", 1)
    mine, back = call(
        tail_body, (z2g, map_row), [((rows, cols), BF), ((rows, cols), BF)], small=0, name="tail"
    )
    ret2 = shifted(back, SUB, -1)
    pack = summed(pack, "sub_0")
    pack = summed(pack, "sub_1")
    pack = jnp.stack([pack, turned(pack, "sub_2", 1)])
    packs = from_others(pack, "help")
    sol, res = call(
        solve_body,
        (counts, pack, *packs, r, im, low, mine, ret2),
        [((rows, cols), F32), ((rows, cols), F32)],
        scratch=[pltpu.VMEM((4, 2, half + 8, half), F32)] + [pltpu.VMEM((cols, cols), F32)] * 5,
        name="solve",
    )
    return sol.reshape(right_side.shape), res.reshape(right_side.shape)


def solution(mesh):
    torus = Mesh(
        mesh.devices.reshape(4, 4, 2, mesh.shape["help"]), ("sub_0", "sub_1", "sub_2", "help")
    )
    in_specs = (P(SUB, "help", None), P(SUB_HELP, None, None), P(SUB_HELP), P(SUB, None), P(SUB))
    out_specs = (P(SUB, "help", None), P(SUB, "help", None))
    return jax.shard_map(
        shards, mesh=torus, in_specs=in_specs, out_specs=out_specs, check_vma=False
    )
```

time: 147 us -> 127 us (0.86)
  Pallas kernels: 43.1 us -> 35.4 us
  waiting for transfers between devices: 52.1 us -> 44.8 us
  local copies, waits for them, and re-layouts: 6.5 us -> 1.91 us
  other arithmetic: 2.27 us -> 0.16 us
  starting transfers between devices: 41.2 us -> 43.1 us
    ppermute x19 -> x20, waiting for transfers between devices: 40.1 us -> 31.8 us  [turned(): lax.ppermute(value, axis, [(i, (i + by) % devices) for i in range(devices)])]
    pallas_call x7 -> x9, Pallas kernels: 43.1 us -> 35.4 us  [call(): pl.pallas_call(body, in_specs=specs, out_specs=[whole() for _ in outs], o...]
    ppermute x19 -> x20, starting transfers between devices: 21.1 us -> 23 us  [turned(): lax.ppermute(value, axis, [(i, (i + by) % devices) for i in range(devices)])]
    unnamed x40 -> x12, local copies, waits for them, and re-layouts: 3.44 us -> 1.62 us
  transfers between devices with their start and end apart: 24 -> 25, of which waited for: 21 -> 20; matrix products, arithmetic and copies ran while one was open for 1% -> 0% of each run, Pallas kernels for 0% -> 0%
where the time goes in v2:
time: 127 us
  waiting for transfers between devices  44.8 us (35%)
  starting transfers between devices  43.1 us (34%)
  Pallas kernels  35.4 us (28%)
  local copies, waits for them, and re-layouts  1.91 us (2%)
  between operations  1.59 us (1%)
    pallas_call x9, Pallas kernels, call(): pl.pallas_call(body, in_specs=specs, out_specs=[whole() for _ in outs], o...  35.4 us
    ppermute x20, waiting for transfers between devices, turned(): lax.ppermute(value, axis, [(i, (i + by) % devices) for i in range(devices)])  31.8 us
    ppermute x20, starting transfers between devices, turned(): lax.ppermute(value, axis, [(i, (i + by) % devices) for i in range(devices)])  23 us
    ppermute x5, starting transfers between devices, shifted(): return lax.ppermute(value, axis, pairs)  20.1 us
    ppermute x5, waiting for transfers between devices, shifted(): return lax.ppermute(value, axis, pairs)  13 us
  transfers between devices with their start and end apart: 25, of which 20 were waited for; matrix products, arithmetic and copies ran while one was open for 0% of the time, Pallas kernels for 0%

profile of v2, /device:TPU:1, one launch (start us, length us, event | category | flops | bytes accessed | tf_op | source)
XLA Modules:
  0.0 126.9 jit_solution(10025213393395598534)
XLA Ops:
  1.4 0.9 copy-done.1
  2.3 0.7 copy-done.4
  3.0 0.6 lower.1.own_ref.w_ref
  3.6 3.6 %collective-permute-start.2 = (bf16[272,256]{1,0:T(8,128)(2,1)S(1)}, bf16[272,256]{1,0:T(8,128)(2,1)S(1)}, u32[]{:S(2)}, u32[]{:S(2)}) collective-permute-start(bf16[272,256]{1,0:T(8,128)(2,1)S(1)} %lower.1.own_ref.w_ref), channel_id=1, source_target_pairs={{0,3},{1,0},{2,1},{3,2},{4,7},{5,4},{6,5},{7,6},{8,11},{9,8},{10,9... | collective-permute-start | bytes 417800 | tf_op jit(solution)/shard_map/ppermute | solution.py:24
  7.5 0.7 collective-permute-start
  8.2 3.4 %collective-permute-start.3 = (s32[512]{0:T(512)}, s32[512]{0:T(512)S(1)}, u32[]{:S(2)}, u32[]{:S(2)}) collective-permute-start(s32[512]{0:T(512)} %bitcast.32), channel_id=1, source_target_pairs={{4,0},{8,4},{12,8},{16,12},{20,16},{24,20},{28,24},{32,28},{36,32}... | collective-permute-start | bytes 6152 | tf_op jit(solution)/shard_map/ppermute | solution.py:19
  11.7 3.3 %collective-permute-done.3 = s32[512]{0:T(512)S(1)} collective-permute-done((s32[512]{0:T(512)}, s32[512]{0:T(512)S(1)}, u32[]{:S(2)}, u32[]{:S(2)}) %collective-permute-start.3) | collective-permute-done | bytes 2080 | tf_op jit(solution)/shard_map/ppermute | solution.py:19
  15.1 2.2 %collective-permute-done.a_ref = bf16[272,256]{1,0:T(8,128)(2,1)S(1)} collective-permute-done((bf16[272,256]{1,0:T(8,128)(2,1)S(1)}, bf16[272,256]{1,0:T(8,128)(2,1)S(1)}, u32[]{:S(2)}, u32[]{:S(2)}) %collective-permute-start) | collective-permute-done | bytes 139296 | tf_op jit(solution)/shard_map/ppermute | solution.py:24
  17.3 0.7 pick.1
  17.9 3.9 %collective-permute-start.4 = (bf16[528,256]{1,0:T(8,128)(2,1)S(1)}, bf16[528,256]{1,0:T(8,128)(2,1)S(1)}, u32[]{:S(2)}, u32[]{:S(2)}) collective-permute-start(bf16[528,256]{1,0:T(8,128)(2,1)S(1)} %get-tuple-element.19), channel_id=1, source_target_pairs={{0,4},{4,8},{8,12},{12,16},{16,20},{20,24},{24,28},{28,32},{32,36}... | collective-permute-start | bytes 811016 | tf_op jit(solution)/shard_map/ppermute | solution.py:19
  21.9 0.4 early.1.early_ref
  22.3 2.9 %collective-permute-done.4.halo_ref.bor_ref = bf16[528,256]{1,0:T(8,128)(2,1)S(1)} collective-permute-done((bf16[528,256]{1,0:T(8,128)(2,1)S(1)}, bf16[528,256]{1,0:T(8,128)(2,1)S(1)}, u32[]{:S(2)}, u32[]{:S(2)}) %collective-permute-start.4) | collective-permute-done | bytes 270368 | tf_op jit(solution)/shard_map/ppermute | solution.py:19
  25.5 0.4 collective-permute-start.7
  25.9 0.3 collective-permute-start.6
  26.2 0.8 collective-permute-start.5
  27.1 4.2 %collective-permute-done.7.c_ref = bf16[384,256]{1,0:T(8,128)(2,1)S(1)} collective-permute-done((bf16[384,256]{1,0:T(8,128)(2,1)S(1)}, bf16[384,256]{1,0:T(8,128)(2,1)S(1)}, u32[]{:S(2)}, u32[]{:S(2)}) %collective-permute-start.7) | collective-permute-done | bytes 196640 | tf_op jit(solution)/shard_map/ppermute | solution.py:24
  31.3 1.8 %collective-permute-done.6.b_ref = bf16[384,256]{1,0:T(8,128)(2,1)S(1)} collective-permute-done((bf16[384,256]{1,0:T(8,128)(2,1)S(1)}, bf16[384,256]{1,0:T(8,128)(2,1)S(1)}, u32[]{:S(2)}, u32[]{:S(2)}) %collective-permute-start.6) | collective-permute-done | bytes 196640 | tf_op jit(solution)/shard_map/ppermute | solution.py:24
  33.2 1.6 %collective-permute-done.5.a_ref = bf16[384,256]{1,0:T(8,128)(2,1)S(1)} collective-permute-done((bf16[384,256]{1,0:T(8,128)(2,1)S(1)}, bf16[384,256]{1,0:T(8,128)(2,1)S(1)}, u32[]{:S(2)}, u32[]{:S(2)}) %collective-permute-start.5) | collective-permute-done | bytes 196640 | tf_op jit(solution)/shard_map/ppermute | solution.py:24
  34.8 1.9 %spread.1 = (bf16[1536,256]{1,0:T(8,128)(2,1)S(1)}, bf16[512,256]{1,0:T(8,128)(2,1)}, bf16[512,256]{1,0:T(8,128)(2,1)}) custom-call(s32[1]{0:T(128)S(6)} %copy.10.count, s32[12]{0:T(128)S(1)} %pad_add_fusion.index, bf16[384,256]{1,0:T(8,128)(2,1)S(1)} %first.1.own_ref, bf16[384,256]{1,0:T(8,128)(2,1)S(1)} %collective-permute-done.5.a_ref, ...), custom_call_target="tpu_custom_call" | custom-call | tf_op jit(solution)/shard_map/spread/pallas_call | solution.py:48
  36.6 1.9 %collective-permute-start.8 = (bf16[512,256]{1,0:T(8,128)(2,1)}, bf16[512,256]{1,0:T(8,128)(2,1)S(1)}, u32[]{:S(2)}, u32[]{:S(2)}) collective-permute-start(bf16[512,256]{1,0:T(8,128)(2,1)} %get-tuple-element.21), channel_id=1, source_target_pairs={{4,0},{8,4},{12,8},{16,12},{20,16},{24,20},{28,24},{32,28},{36,32}... | collective-permute-start | bytes 786440 | tf_op jit(solution)/shard_map/ppermute | solution.py:19
  38.5 7.6 %collective-permute-start.9 = (bf16[512,256]{1,0:T(8,128)(2,1)}, bf16[512,256]{1,0:T(8,128)(2,1)}, u32[]{:S(2)}, u32[]{:S(2)}) collective-permute-start(bf16[512,256]{1,0:T(8,128)(2,1)} %get-tuple-element.22), channel_id=1, source_target_pairs={{0,4},{4,8},{8,12},{12,16},{16,20},{20,24},{24,28},{28,32},{32,36}... | collective-permute-start | bytes 786440 | tf_op jit(solution)/shard_map/ppermute | solution.py:19
  46.3 2.5 %collective-permute-done.8.ret_ref = bf16[512,256]{1,0:T(8,128)(2,1)S(1)} collective-permute-done((bf16[512,256]{1,0:T(8,128)(2,1)}, bf16[512,256]{1,0:T(8,128)(2,1)S(1)}, u32[]{:S(2)}, u32[]{:S(2)}) %collective-permute-start.8) | collective-permute-done | bytes 262176 | tf_op jit(solution)/shard_map/ppermute | solution.py:19
  48.7 1.0 collective-permute-done.9.zp_ref
  49.7 2.2 %second.1 = (bf16[384,256]{1,0:T(8,128)(2,1)S(1)}, f32[1024,256]{1,0:T(8,128)S(1)}, bf16[1024,256]{1,0:T(8,128)(2,1)S(1)}, bf16[512,256]{1,0:T(8,128)(2,1)S(1)}) custom-call(s32[1]{0:T(128)S(6)} %copy.10.count, bf16[384,1536]{1,0:T(8,128)(2,1)S(1)} %bitcast.27, bf16[1536,256]{1,0:T(8,128)(2,1)S(1)} %get-tuple-element.20.zg_ref, ...), custom_call_target="tpu_custom_call" | custom-call | tf_op jit(solution)/shard_map/second/pallas_call | solution.py:48
  52.0 0.7 collective-permute-start.12
  52.6 0.8 collective-permute-start.10
  53.5 3.1 %collective-permute-done.12.c_ref = bf16[384,256]{1,0:T(8,128)(2,1)S(1)} collective-permute-done((bf16[384,256]{1,0:T(8,128)(2,1)S(1)}, bf16[384,256]{1,0:T(8,128)(2,1)S(1)}, u32[]{:S(2)}, u32[]{:S(2)}) %collective-permute-start.12) | collective-permute-done | bytes 196640 | tf_op jit(solution)/shard_map/ppermute | solution.py:24
  56.5 2.2 %collective-permute-done.11.b_ref = bf16[384,256]{1,0:T(8,128)(2,1)S(1)} collective-permute-done((bf16[384,256]{1,0:T(8,128)(2,1)S(1)}, bf16[384,256]{1,0:T(8,128)(2,1)S(1)}, u32[]{:S(2)}, u32[]{:S(2)}) %collective-permute-start.11) | collective-permute-done | bytes 196640 | tf_op jit(solution)/shard_map/ppermute | solution.py:24
  58.7 2.0 %collective-permute-done.10.a_ref = bf16[384,256]{1,0:T(8,128)(2,1)S(1)} collective-permute-done((bf16[384,256]{1,0:T(8,128)(2,1)S(1)}, bf16[384,256]{1,0:T(8,128)(2,1)S(1)}, u32[]{:S(2)}, u32[]{:S(2)}) %collective-permute-start.10) | collective-permute-done | bytes 196640 | tf_op jit(solution)/shard_map/ppermute | solution.py:24
  60.8 1.1 gram.1
  61.9 1.2 collective-permute-done.13
  63.2 7.1 %collective-permute-start.16 = (f32[136,128]{1,0:T(8,128)S(1)}, f32[136,128]{1,0:T(8,128)S(1)}, u32[]{:S(2)}, u32[]{:S(2)}) collective-permute-start(f32[136,128]{1,0:T(8,128)S(1)} %add.21), channel_id=1, source_target_pairs={{0,96},{32,0},{64,32},{96,64},{1,97},{33,1},{65,33},{97,65},{2,98}... | collective-permute-start | bytes 208904 | tf_op jit(solution)/shard_map/ppermute | solution.py:24
  70.3 0.5 collective-permute-start.15
  70.8 0.6 collective-permute-start.14
  71.7 3.3 %collective-permute-done.15 = f32[136,128]{1,0:T(8,128)S(1)} collective-permute-done((f32[136,128]{1,0:T(8,128)S(1)}, f32[136,128]{1,0:T(8,128)S(1)}, u32[]{:S(2)}, u32[]{:S(2)}) %collective-permute-start.15) | collective-permute-done | bytes 69664 | tf_op jit(solution)/shard_map/ppermute | solution.py:24
  75.0 1.9 %collective-permute-done.14 = f32[136,128]{1,0:T(8,128)S(1)} collective-permute-done((f32[136,128]{1,0:T(8,128)S(1)}, f32[136,128]{1,0:T(8,128)S(1)}, u32[]{:S(2)}, u32[]{:S(2)}) %collective-permute-start.14) | collective-permute-done | bytes 69664 | tf_op jit(solution)/shard_map/ppermute | solution.py:24
  77.3 2.8 %collective-permute-start.18 = (f32[136,128]{1,0:T(8,128)S(1)}, f32[136,128]{1,0:T(8,128)S(1)}, u32[]{:S(2)}, u32[]{:S(2)}) collective-permute-start(f32[136,128]{1,0:T(8,128)S(1)} %add_add_fusion.1), channel_id=1, source_target_pairs={{0,16},{8,24},{16,0},{24,8},{1,17},{9,25},{17,1},{25,9},{2,18},{10... | collective-permute-start | bytes 208904 | tf_op jit(solution)/shard_map/ppermute | solution.py:24
  80.2 1.7 %collective-permute-done.18 = f32[136,128]{1,0:T(8,128)S(1)} collective-permute-done((f32[136,128]{1,0:T(8,128)S(1)}, f32[136,128]{1,0:T(8,128)S(1)}, u32[]{:S(2)}, u32[]{:S(2)}) %collective-permute-start.18) | collective-permute-done | bytes 69664 | tf_op jit(solution)/shard_map/ppermute | solution.py:24
  81.9 3.3 %collective-permute-done.17 = f32[136,128]{1,0:T(8,128)S(1)} collective-permute-done((f32[136,128]{1,0:T(8,128)S(1)}, f32[136,128]{1,0:T(8,128)S(1)}, u32[]{:S(2)}, u32[]{:S(2)}) %collective-permute-start.17) | collective-permute-done | bytes 69664 | tf_op jit(solution)/shard_map/ppermute | solution.py:24
  85.2 2.0 %collective-permute-start.20 = (f32[136,128]{1,0:T(8,128)S(1)}, f32[136,128]{1,0:T(8,128)S(1)}, u32[]{:S(2)}, u32[]{:S(2)}) collective-permute-start(f32[136,128]{1,0:T(8,128)S(1)} %add_add_fusion), channel_id=1, source_target_pairs={{0,4},{4,0},{1,5},{5,1},{2,6},{6,2},{3,7},{7,3},{8,12},{12,8},{9,1... | collective-permute-start | bytes 208904 | tf_op jit(solution)/shard_map/ppermute | solution.py:24
  87.3 0.9 collective-permute-done.20
  88.2 0.5 collective-permute-start.23
  88.7 0.5 collective-permute-start.22
  89.2 0.6 collective-permute-start.21
  90.0 3.3 %collective-permute-start.24 = (bf16[256,256]{1,0:T(8,128)(2,1)S(1)}, bf16[256,256]{1,0:T(8,128)(2,1)S(1)}, u32[]{:S(2)}, u32[]{:S(2)}) collective-permute-start(bf16[256,256]{1,0:T(8,128)(2,1)S(1)} %get-tuple-element.31), channel_id=1, source_target_pairs={{4,0},{8,4},{12,8},{16,12},{20,16},{24,20},{28,24},{32,28},{36,32}... | collective-permute-start | bytes 393224 | tf_op jit(solution)/shard_map/ppermute | solution.py:19
  93.3 3.3 %collective-permute-done.24.ret_ref = bf16[256,256]{1,0:T(8,128)(2,1)S(1)} collective-permute-done((bf16[256,256]{1,0:T(8,128)(2,1)S(1)}, bf16[256,256]{1,0:T(8,128)(2,1)S(1)}, u32[]{:S(2)}, u32[]{:S(2)}) %collective-permute-start.24) | collective-permute-done | bytes 131104 | tf_op jit(solution)/shard_map/ppermute | solution.py:19
  96.6 2.2 %collective-permute-done.21.a_ref = f32[2,136,128]{2,1,0:T(8,128)S(1)} collective-permute-done((f32[2,136,128]{2,1,0:T(8,128)S(1)}, f32[2,136,128]{2,1,0:T(8,128)S(1)}, u32[]{:S(2)}, u32[]{:S(2)}) %collective-permute-start.21) | collective-permute-done | bytes 139296 | tf_op jit(solution)/shard_map/ppermute | solution.py:24
  98.7 28.1 %solve.1 = (f32[256,256]{1,0:T(8,128)}, f32[256,256]{1,0:T(8,128)}) custom-call(s32[1]{0:T(128)S(6)} %copy.10.count, f32[2,136,128]{2,1,0:T(8,128)S(1)} %pad_maximum_fusion.own_ref, f32[2,136,128]{2,1,0:T(8,128)S(1)} %collective-permute-done.21.a_ref, f32[2,136,128]{2,1,0:T(8,128)S(1)} %collective-permute-done.22.b_ref, ...), custom_call_target="tpu_custom_call" | custom-call | tf_op jit(solution)/shard_map/solve/pallas_call | solution.py:48
  (33 shorter events, 2.2 us)
Async XLA Ops:
  0.6 21.3 %copy-start = (bf16[3,128,1536]{2,1,0:T(8,128)(2,1)S(1)}, bf16[3,128,1536]{2,1,0:T(8,128)(2,1)}, u32[]{:S(2)}) copy-start(bf16[3,128,1536]{2,1,0:T(8,128)(2,1)} %param.6) | copy-start | bytes 3538948
  1.4 1.0 copy-start.1
  2.3 0.7 copy-start.4
  3.6 11.5 %collective-permute-start.2 = (bf16[272,256]{1,0:T(8,128)(2,1)S(1)}, bf16[272,256]{1,0:T(8,128)(2,1)S(1)}, u32[]{:S(2)}, u32[]{:S(2)}) collective-permute-start(bf16[272,256]{1,0:T(8,128)(2,1)S(1)} %lower.1.own_ref.w_ref), channel_id=1, source_target_pairs={{0,3},{1,0},{2,1},{3,2},{4,7},{5,4},{6,5},{7,6},{8,11},{9,8},{10,9... | collective-permute-start | bytes 417800 | tf_op jit(solution)/shard_map/ppermute | solution.py:24
  7.2 7.9 %collective-permute-start.1 = (bf16[272,256]{1,0:T(8,128)(2,1)S(1)}, bf16[272,256]{1,0:T(8,128)(2,1)S(1)}, u32[]{:S(2)}, u32[]{:S(2)}) collective-permute-start(bf16[272,256]{1,0:T(8,128)(2,1)S(1)} %lower.1.own_ref.w_ref), channel_id=1, source_target_pairs={{0,2},{1,3},{2,0},{3,1},{4,6},{5,7},{6,4},{7,5},{8,10},{9,11},{10,... | collective-permute-start | bytes 417800 | tf_op jit(solution)/shard_map/ppermute | solution.py:24
  7.5 9.7 %collective-permute-start = (bf16[272,256]{1,0:T(8,128)(2,1)S(1)}, bf16[272,256]{1,0:T(8,128)(2,1)S(1)}, u32[]{:S(2)}, u32[]{:S(2)}) collective-permute-start(bf16[272,256]{1,0:T(8,128)(2,1)S(1)} %lower.1.own_ref.w_ref), channel_id=1, source_target_pairs={{0,1},{1,2},{2,3},{3,0},{4,5},{5,6},{6,7},{7,4},{8,9},{9,10},{10,1... | collective-permute-start | bytes 417800 | tf_op jit(solution)/shard_map/ppermute | solution.py:24
  8.2 6.7 %collective-permute-start.3 = (s32[512]{0:T(512)}, s32[512]{0:T(512)S(1)}, u32[]{:S(2)}, u32[]{:S(2)}) collective-permute-start(s32[512]{0:T(512)} %bitcast.32), channel_id=1, source_target_pairs={{4,0},{8,4},{12,8},{16,12},{20,16},{24,20},{28,24},{32,28},{36,32}... | collective-permute-start | bytes 6152 | tf_op jit(solution)/shard_map/ppermute | solution.py:19
  17.9 7.3 %collective-permute-start.4 = (bf16[528,256]{1,0:T(8,128)(2,1)S(1)}, bf16[528,256]{1,0:T(8,128)(2,1)S(1)}, u32[]{:S(2)}, u32[]{:S(2)}) collective-permute-start(bf16[528,256]{1,0:T(8,128)(2,1)S(1)} %get-tuple-element.19), channel_id=1, source_target_pairs={{0,4},{4,8},{8,12},{12,16},{16,20},{20,24},{24,28},{28,32},{32,36}... | collective-permute-start | bytes 811016 | tf_op jit(solution)/shard_map/ppermute | solution.py:19
  22.3 4.8 %copy-start.5 = (s32[3]{0:T(128)S(1)}, s32[3]{0:T(128)}, u32[]{:S(2)}) copy-start(s32[3]{0:T(128)} %index.1) | copy-start | bytes 40
  22.3 23.8 %copy-start.3 = (s32[1,512]{1,0:T(1,128)S(1)}, s32[1,512]{1,0:T(1,128)}, u32[]{:S(2)}) copy-start(s32[1,512]{1,0:T(1,128)} %map_ref.1) | copy-start | bytes 6148
  25.5 5.8 %collective-permute-start.7 = (bf16[384,256]{1,0:T(8,128)(2,1)S(1)}, bf16[384,256]{1,0:T(8,128)(2,1)S(1)}, u32[]{:S(2)}, u32[]{:S(2)}) collective-permute-start(bf16[384,256]{1,0:T(8,128)(2,1)S(1)} %first.1.own_ref), channel_id=1, source_target_pairs={{0,3},{1,0},{2,1},{3,2},{4,7},{5,4},{6,5},{7,6},{8,11},{9,8},{10,9... | collective-permute-start | bytes 589832 | tf_op jit(solution)/shard_map/ppermute | solution.py:24
  25.9 7.3 %collective-permute-start.6 = (bf16[384,256]{1,0:T(8,128)(2,1)S(1)}, bf16[384,256]{1,0:T(8,128)(2,1)S(1)}, u32[]{:S(2)}, u32[]{:S(2)}) collective-permute-start(bf16[384,256]{1,0:T(8,128)(2,1)S(1)} %first.1.own_ref), channel_id=1, source_target_pairs={{0,2},{1,3},{2,0},{3,1},{4,6},{5,7},{6,4},{7,5},{8,10},{9,11},{10,... | collective-permute-start | bytes 589832 | tf_op jit(solution)/shard_map/ppermute | solution.py:24
  26.2 8.6 %collective-permute-start.5 = (bf16[384,256]{1,0:T(8,128)(2,1)S(1)}, bf16[384,256]{1,0:T(8,128)(2,1)S(1)}, u32[]{:S(2)}, u32[]{:S(2)}) collective-permute-start(bf16[384,256]{1,0:T(8,128)(2,1)S(1)} %first.1.own_ref), channel_id=1, source_target_pairs={{0,1},{1,2},{2,3},{3,0},{4,5},{5,6},{6,7},{7,4},{8,9},{9,10},{10,1... | collective-permute-start | bytes 589832 | tf_op jit(solution)/shard_map/ppermute | solution.py:24
  36.6 12.1 %collective-permute-start.8 = (bf16[512,256]{1,0:T(8,128)(2,1)}, bf16[512,256]{1,0:T(8,128)(2,1)S(1)}, u32[]{:S(2)}, u32[]{:S(2)}) collective-permute-start(bf16[512,256]{1,0:T(8,128)(2,1)} %get-tuple-element.21), channel_id=1, source_target_pairs={{4,0},{8,4},{12,8},{16,12},{20,16},{24,20},{28,24},{32,28},{36,32}... | collective-permute-start | bytes 786440 | tf_op jit(solution)/shard_map/ppermute | solution.py:19
  38.5 11.2 %collective-permute-start.9 = (bf16[512,256]{1,0:T(8,128)(2,1)}, bf16[512,256]{1,0:T(8,128)(2,1)}, u32[]{:S(2)}, u32[]{:S(2)}) collective-permute-start(bf16[512,256]{1,0:T(8,128)(2,1)} %get-tuple-element.22), channel_id=1, source_target_pairs={{0,4},{4,8},{8,12},{12,16},{16,20},{20,24},{24,28},{28,32},{32,36}... | collective-permute-start | bytes 786440 | tf_op jit(solution)/shard_map/ppermute | solution.py:19
  52.0 4.6 %collective-permute-start.12 = (bf16[384,256]{1,0:T(8,128)(2,1)S(1)}, bf16[384,256]{1,0:T(8,128)(2,1)S(1)}, u32[]{:S(2)}, u32[]{:S(2)}) collective-permute-start(bf16[384,256]{1,0:T(8,128)(2,1)S(1)} %get-tuple-element.23.own_ref), channel_id=1, source_target_pairs={{0,3},{1,0},{2,1},{3,2},{4,7},{5,4},{6,5},{7,6},{8,11},{9,8},{10,9... | collective-permute-start | bytes 589832 | tf_op jit(solution)/shard_map/ppermute | solution.py:24
  52.6 6.1 %collective-permute-start.11 = (bf16[384,256]{1,0:T(8,128)(2,1)S(1)}, bf16[384,256]{1,0:T(8,128)(2,1)S(1)}, u32[]{:S(2)}, u32[]{:S(2)}) collective-permute-start(bf16[384,256]{1,0:T(8,128)(2,1)S(1)} %get-tuple-element.23.own_ref), channel_id=1, source_target_pairs={{0,2},{1,3},{2,0},{3,1},{4,6},{5,7},{6,4},{7,5},{8,10},{9,11},{10,... | collective-permute-start | bytes 589832 | tf_op jit(solution)/shard_map/ppermute | solution.py:24
  52.6 8.1 %collective-permute-start.10 = (bf16[384,256]{1,0:T(8,128)(2,1)S(1)}, bf16[384,256]{1,0:T(8,128)(2,1)S(1)}, u32[]{:S(2)}, u32[]{:S(2)}) collective-permute-start(bf16[384,256]{1,0:T(8,128)(2,1)S(1)} %get-tuple-element.23.own_ref), channel_id=1, source_target_pairs={{0,1},{1,2},{2,3},{3,0},{4,5},{5,6},{6,7},{7,4},{8,9},{9,10},{10,1... | collective-permute-start | bytes 589832 | tf_op jit(solution)/shard_map/ppermute | solution.py:24
  61.8 36.9 %copy-start.2 = (f32[1,256,256]{2,1,0:T(8,128)S(1)}, f32[1,256,256]{2,1,0:T(8,128)}, u32[]{:S(2)}) copy-start(f32[1,256,256]{2,1,0:T(8,128)} %param.5) | copy-start | bytes 786436
  61.8 1.3 %collective-permute-start.13 = (f32[136,128]{1,0:T(8,128)S(1)}, f32[136,128]{1,0:T(8,128)S(1)}, u32[]{:S(2)}, u32[]{:S(2)}) collective-permute-start(f32[136,128]{1,0:T(8,128)S(1)} %get-tuple-element.28), channel_id=1, source_target_pairs={{0,4},{4,0},{1,5},{5,1},{2,6},{6,2},{3,7},{7,3},{8,12},{12,8},{9,1... | collective-permute-start | bytes 208904 | tf_op jit(solution)/shard_map/ppermute | solution.py:24
  63.2 8.5 %collective-permute-start.16 = (f32[136,128]{1,0:T(8,128)S(1)}, f32[136,128]{1,0:T(8,128)S(1)}, u32[]{:S(2)}, u32[]{:S(2)}) collective-permute-start(f32[136,128]{1,0:T(8,128)S(1)} %add.21), channel_id=1, source_target_pairs={{0,96},{32,0},{64,32},{96,64},{1,97},{33,1},{65,33},{97,65},{2,98}... | collective-permute-start | bytes 208904 | tf_op jit(solution)/shard_map/ppermute | solution.py:24
  70.3 4.7 %collective-permute-start.15 = (f32[136,128]{1,0:T(8,128)S(1)}, f32[136,128]{1,0:T(8,128)S(1)}, u32[]{:S(2)}, u32[]{:S(2)}) collective-permute-start(f32[136,128]{1,0:T(8,128)S(1)} %add.21), channel_id=1, source_target_pairs={{0,64},{32,96},{64,0},{96,32},{1,65},{33,97},{65,1},{97,33},{2,66}... | collective-permute-start | bytes 208904 | tf_op jit(solution)/shard_map/ppermute | solution.py:24
  70.8 6.1 %collective-permute-start.14 = (f32[136,128]{1,0:T(8,128)S(1)}, f32[136,128]{1,0:T(8,128)S(1)}, u32[]{:S(2)}, u32[]{:S(2)}) collective-permute-start(f32[136,128]{1,0:T(8,128)S(1)} %add.21), channel_id=1, source_target_pairs={{0,32},{32,64},{64,96},{96,0},{1,33},{33,65},{65,97},{97,1},{2,34}... | collective-permute-start | bytes 208904 | tf_op jit(solution)/shard_map/ppermute | solution.py:24
  76.9 3.3 %collective-permute-start.19 = (f32[136,128]{1,0:T(8,128)S(1)}, f32[136,128]{1,0:T(8,128)S(1)}, u32[]{:S(2)}, u32[]{:S(2)}) collective-permute-start(f32[136,128]{1,0:T(8,128)S(1)} %add_add_fusion.1), channel_id=1, source_target_pairs={{0,24},{8,0},{16,8},{24,16},{1,25},{9,1},{17,9},{25,17},{2,26},{10... | collective-permute-start | bytes 208904 | tf_op jit(solution)/shard_map/ppermute | solution.py:24
  77.3 4.7 %collective-permute-start.18 = (f32[136,128]{1,0:T(8,128)S(1)}, f32[136,128]{1,0:T(8,128)S(1)}, u32[]{:S(2)}, u32[]{:S(2)}) collective-permute-start(f32[136,128]{1,0:T(8,128)S(1)} %add_add_fusion.1), channel_id=1, source_target_pairs={{0,16},{8,24},{16,0},{24,8},{1,17},{9,25},{17,1},{25,9},{2,18},{10... | collective-permute-start | bytes 208904 | tf_op jit(solution)/shard_map/ppermute | solution.py:24
  80.1 5.1 %collective-permute-start.17 = (f32[136,128]{1,0:T(8,128)S(1)}, f32[136,128]{1,0:T(8,128)S(1)}, u32[]{:S(2)}, u32[]{:S(2)}) collective-permute-start(f32[136,128]{1,0:T(8,128)S(1)} %add_add_fusion.1), channel_id=1, source_target_pairs={{0,8},{8,16},{16,24},{24,0},{1,9},{9,17},{17,25},{25,1},{2,10},{10... | collective-permute-start | bytes 208904 | tf_op jit(solution)/shard_map/ppermute | solution.py:24
  85.2 3.0 %collective-permute-start.20 = (f32[136,128]{1,0:T(8,128)S(1)}, f32[136,128]{1,0:T(8,128)S(1)}, u32[]{:S(2)}, u32[]{:S(2)}) collective-permute-start(f32[136,128]{1,0:T(8,128)S(1)} %add_add_fusion), channel_id=1, source_target_pairs={{0,4},{4,0},{1,5},{5,1},{2,6},{6,2},{3,7},{7,3},{8,12},{12,8},{9,1... | collective-permute-start | bytes 208904 | tf_op jit(solution)/shard_map/ppermute | solution.py:24
  88.2 8.4 %collective-permute-start.23 = (f32[2,136,128]{2,1,0:T(8,128)S(1)}, f32[2,136,128]{2,1,0:T(8,128)S(1)}, u32[]{:S(2)}, u32[]{:S(2)}) collective-permute-start(f32[2,136,128]{2,1,0:T(8,128)S(1)} %pad_maximum_fusion.own_ref), channel_id=1, source_target_pairs={{0,3},{1,0},{2,1},{3,2},{4,7},{5,4},{6,5},{7,6},{8,11},{9,8},{10,9... | collective-permute-start | bytes 417800 | tf_op jit(solution)/shard_map/ppermute | solution.py:24
  88.7 7.9 %collective-permute-start.22 = (f32[2,136,128]{2,1,0:T(8,128)S(1)}, f32[2,136,128]{2,1,0:T(8,128)S(1)}, u32[]{:S(2)}, u32[]{:S(2)}) collective-permute-start(f32[2,136,128]{2,1,0:T(8,128)S(1)} %pad_maximum_fusion.own_ref), channel_id=1, source_target_pairs={{0,2},{1,3},{2,0},{3,1},{4,6},{5,7},{6,4},{7,5},{8,10},{9,11},{10,... | collective-permute-start | bytes 417800 | tf_op jit(solution)/shard_map/ppermute | solution.py:24
  89.2 9.6 %collective-permute-start.21 = (f32[2,136,128]{2,1,0:T(8,128)S(1)}, f32[2,136,128]{2,1,0:T(8,128)S(1)}, u32[]{:S(2)}, u32[]{:S(2)}) collective-permute-start(f32[2,136,128]{2,1,0:T(8,128)S(1)} %pad_maximum_fusion.own_ref), channel_id=1, source_target_pairs={{0,1},{1,2},{2,3},{3,0},{4,5},{5,6},{6,7},{7,4},{8,9},{9,10},{10,1... | collective-permute-start | bytes 417800 | tf_op jit(solution)/shard_map/ppermute | solution.py:24
  90.0 6.6 %collective-permute-start.24 = (bf16[256,256]{1,0:T(8,128)(2,1)S(1)}, bf16[256,256]{1,0:T(8,128)(2,1)S(1)}, u32[]{:S(2)}, u32[]{:S(2)}) collective-permute-start(bf16[256,256]{1,0:T(8,128)(2,1)S(1)} %get-tuple-element.31), channel_id=1, source_target_pairs={{4,0},{8,4},{12,8},{16,12},{20,16},{24,20},{28,24},{32,28},{36,32}... | collective-permute-start | bytes 393224 | tf_op jit(solution)/shard_map/ppermute | solution.py:19

commit v3 on v2

--- a/solution.py
+++ b/solution.py
@@ -13,12 +13,6 @@
 F32 = jnp.float32
 
 
-def shifted(value, axis, by):
-    devices = lax.axis_size(axis)
-    pairs = [(i, i + by) for i in range(devices) if 0 <= i + by < devices]
-    return lax.ppermute(value, axis, pairs)
-
-
 def turned(value, axis, by):
     devices = lax.axis_size(axis)
     return lax.ppermute(value, axis, [(i, (i + by) % devices) for i in range(devices)])
@@ -43,12 +37,12 @@
     return pl.BlockSpec(memory_space=pltpu.MemorySpace.SMEM)
 
 
-def call(body, args, outs, scratch=(), small=1, name=None):
+def call(body, args, outs, scratch=(), small=1, name=None, tail=None):
     specs = [scalars()] * small + [whole()] * (len(args) - small)
     return pl.pallas_call(
         body,
         in_specs=specs,
-        out_specs=[whole() for _ in outs],
+        out_specs=[whole() for _ in outs[1:]] + [tail or whole()],
         out_shape=[jax.ShapeDtypeStruct(s, d) for s, d in outs],
         scratch_shapes=list(scratch),
         compiler_params=pltpu.CompilerParams(vmem_limit_bytes=16 << 20),
@@ -91,53 +85,94 @@
     return lax.axis_index("help")
 
 
-def lower_body(count, index, r_ref, out_ref):
-    rows = r_ref.shape[0]
-    cols = r_ref.shape[1]
-    row = iota((rows, 1), 0) + here() * rows
-    out_ref[:rows, :] = jnp.where(row < count[0], r_ref[...], 0.0).astype(BF)
-    col = iota((16, cols), 1)
-    info = jnp.zeros((16, cols), F32)
-    values = [index[0], index[1], index[2], count[0] // 32, count[0] % 32]
+def has_previous():
+    return lax.axis_index(SUB) > 0
+
+
+def has_next():
+    return lax.axis_index(SUB) + 1 < lax.axis_size(SUB)
+
+
+def weight(flag):
+    return flag.astype(jnp.int32).astype(F32)
+
+
+def blocks_of(*blocks):
+    return tuple((block, k, 0) for k, block in enumerate(blocks))
+
+
+def pick_body(own_ref, a_ref, b_ref, c_ref, later_ref, wg_ref, pick_ref):
+    rows = own_ref.shape[0]
+    for ref, k, start in blocks_of(own_ref, a_ref, b_ref, c_ref):
+        at = pl.multiple_of(lax.rem(here() + 4 - k, 4) * rows + start, 16)
+        wg_ref[pl.ds(at, ref.shape[0]), :] = ref[...]
+    choose = hot(later_ref[...] == iota((later_ref.shape[0], wg_ref.shape[0]), 1))
+    pick_ref[...] = mm(choose, wg_ref[...]).astype(BF)
+
+
+def numbers(shape, values):
+    col = iota(shape, 1)
+    info = jnp.zeros(shape, F32)
     for k, value in enumerate(values):
         info = jnp.where(col == k, value.astype(F32), info)
-    out_ref[rows:, :] = info.astype(BF)
-
-
-def pick_body(own_ref, a_ref, b_ref, c_ref, later_ref, wg_ref, pick_ref):
+    return info.astype(BF)
+
+
+def number(row, at):
+    return jnp.sum(jnp.where(iota(row.shape, 1) == at, row, 0.0)).astype(jnp.int32)
+
+
+def place(pieces, rows, panel, tables, out_ref):
+    for ref, k, start in pieces:
+        at = start
+        stop = min(start + ref.shape[0], rows)
+        while at < stop:
+            slot = at // panel
+            end = min((slot + 1) * panel, stop)
+            to = tables[k][slot] * panel + at % panel
+            out_ref[pl.ds(pl.multiple_of(to, 16), end - at), :] = ref[at - start : end - start, :]
+            at = end
+
+
+def tables_of(index, pieces, rows):
+    tables = [[index[0], index[1], index[2]], None, None, None]
+    for ref, k, start in pieces[1:]:
+        if start + ref.shape[0] > rows:
+            row = ref[rows - start : rows - start + 1, :].astype(F32)
+            tables[k] = [number(row, j) for j in range(3)]
+    return tables
+
+
+def early_body(index, f_ref, wg_ref, z_ref, info_ref):
+    z_ref[...] = mm(f_ref[:, : wg_ref.shape[0]], wg_ref[...])
+    info_ref[...] = numbers(info_ref.shape, [index[0], index[1], index[2]])
+
+
+def first_body(f_ref, early_ref, info_ref, halo_ref, z_ref):
+    rows = early_ref.shape[0]
+    owned = f_ref.shape[1] - halo_ref.shape[0]
+    from_halo = mm(f_ref[:, owned:], halo_ref[...])
+    z_ref[:rows, :] = (early_ref[...] - weight(has_previous()) * from_halo).astype(BF)
+    z_ref[rows:, :] = info_ref[...]
+
+
+def spread_body(
+    count, index, own_ref, a_ref, b_ref, c_ref, later_ref, zg_ref, halo_ref, pick_ref, table_ref
+):
     rows = own_ref.shape[0] - 16
-    h = here()
-    for k, ref in enumerate((own_ref, a_ref, b_ref, c_ref)):
-        at = pl.multiple_of(lax.rem(h + 4 - k, 4) * rows, rows)
-        wg_ref[pl.ds(at, rows), :] = ref[:rows, :]
-    halo = later_ref.shape[0]
-    choose = hot(later_ref[...] == iota((halo, wg_ref.shape[0]), 1))
-    pick_ref[:halo, :] = mm(choose, wg_ref[...]).astype(BF)
-    pick_ref[halo:, :] = own_ref[rows:, :]
-
-
-def early_body(f_ref, wg_ref, z_ref):
-    z_ref[...] = mm(f_ref[:, : wg_ref.shape[0]], wg_ref[...])
-
-
-def first_body(f_ref, early_ref, halo_ref, z_ref):
-    halo = halo_ref.shape[0] - 16
-    owned = f_ref.shape[1] - halo
-    z_ref[...] = (early_ref[...] - mm(f_ref[:, owned:], halo_ref[:halo, :])).astype(BF)
-
-
-def spread_body(count, index, own_ref, a_ref, b_ref, c_ref, later_ref, zg_ref, halo_ref, pick_ref):
-    panel = own_ref.shape[0] // 3
-    for k, ref in enumerate((own_ref, a_ref, b_ref, c_ref)):
+    pieces = blocks_of(own_ref, a_ref, b_ref, c_ref)
+    tables = tables_of(index, pieces, rows)
+    place(pieces, rows, rows // 3, tables, zg_ref)
+    for k in range(4):
         for j in range(3):
-            at = pl.multiple_of(index[3 * k + j] * panel, panel)
-            zg_ref[pl.ds(at, panel), :] = ref[j * panel : (j + 1) * panel, :]
+            table_ref[3 * k + j] = tables[k][j]
     halo = halo_ref.shape[0]
     owned = zg_ref.shape[0] - halo
     halo_ref[...] = zg_ref[owned:, :]
     later = later_ref[...]
     choose = hot((later == iota((halo, owned), 1)) & (later < count[0]))
-    pick_ref[...] = mm(choose, zg_ref[:owned, :]).astype(BF)
+    pick_ref[:halo, :] = mm(choose, zg_ref[:owned, :]).astype(BF)
+    pick_ref[halo:, :] = numbers((16, zg_ref.shape[1]), [count[0] // 32, count[0] % 32])
 
 
 def second_body(
@@ -147,18 +182,18 @@
     halo = ret_ref.shape[0]
     live = iota((owned, 1), 0) < count[0]
     back = mm(hot(iota((owned, halo), 0) == later_ref[...]), ret_ref[...])
-    image = jnp.where(live, zg_ref[:owned, :].astype(F32) - back, 0.0)
+    image = jnp.where(live, zg_ref[:owned, :].astype(F32) - weight(has_next()) * back, 0.0)
     im_ref[...] = image
     vb = (image - SHIFT * wg_ref[...].astype(F32)).astype(BF)
     vb_ref[...] = vb
-    info = bor_ref[halo : halo + 1, :].astype(F32)
+    info = zp_ref[halo : halo + 1, :].astype(F32)
     lane = iota(info.shape, 1)
-    weight = jnp.where(lane == 3, 32.0, jnp.where(lane == 4, 1.0, 0.0))
-    before = jnp.sum(info * weight, axis=1, keepdims=True)
-    alive = (map_ref[...].astype(F32) < before) & (lax.axis_index(SUB) > 0)
-    term = zp_ref[...].astype(F32) - zg_ref[owned:, :].astype(F32)
-    vh = jnp.where(alive, term, 0.0) - SHIFT * bor_ref[:halo, :].astype(F32)
-    vh = vh.astype(BF)
+    parts = jnp.where(lane == 0, 32.0, jnp.where(lane == 1, 1.0, 0.0))
+    before = jnp.sum(info * parts, axis=1, keepdims=True)
+    alive = map_ref[...].astype(F32) < before
+    term = zp_ref[:halo, :].astype(F32) - zg_ref[owned:, :].astype(F32)
+    vh = jnp.where(alive, term, 0.0) - SHIFT * bor_ref[...].astype(F32)
+    vh = (weight(has_previous()) * vh).astype(BF)
     vh_ref[...] = vh
     z = mm(f_ref[:, :owned], vb) - mm(f_ref[:, owned:], vh)
     z_ref[...] = z.astype(BF)
@@ -168,13 +203,10 @@
     index, own_ref, a_ref, b_ref, c_ref, wg_ref, bor_ref, zg_ref, im_ref, vb_ref, vh_ref,
     keep_ref, give_ref, z2_ref, gram_ref, pack_ref,
 ):
-    panel = own_ref.shape[0] // 3
-    for k, ref in enumerate((own_ref, a_ref, b_ref, c_ref)):
-        for j in range(3):
-            at = pl.multiple_of(index[3 * k + j] * panel, panel)
-            z2_ref[pl.ds(at, panel), :] = ref[j * panel : (j + 1) * panel, :]
+    rows = own_ref.shape[0]
+    tables = [[index[3 * k + j] for j in range(3)] for k in range(4)]
+    place(blocks_of(own_ref, a_ref, b_ref, c_ref), rows, rows // 3, tables, z2_ref)
     owned = wg_ref.shape[0]
-    halo = vh_ref.shape[0]
     h = here()
 
     @pl.when(h == 0)
@@ -183,7 +215,8 @@
 
     @pl.when(h == 1)
     def _():
-        gram_ref[...] = tmm(wg_ref[...], zg_ref[:owned, :]) - tmm(bor_ref[:halo, :], zg_ref[owned:, :])
+        from_halo = tmm(bor_ref[...], zg_ref[owned:, :])
+        gram_ref[...] = tmm(wg_ref[...], zg_ref[:owned, :]) - weight(has_previous()) * from_halo
 
     @pl.when(h == 2)
     def _():
@@ -271,15 +304,15 @@
 
 
 def solve_body(
-    count, own_ref, a_ref, b_ref, c_ref, r_ref, im_ref, w_ref, mine_ref, ret_ref,
+    count, own_ref, other_ref, r_ref, im_ref, w_ref, mine_ref, ret_ref,
     sol_ref, res_ref, pack_ref, g00_ref, g01_ref, g11_ref, gvv_ref, x_ref,
 ):
     h = here()
     core = lax.axis_index("sub_2")
-    for k, ref in enumerate((own_ref, a_ref, b_ref, c_ref)):
+    for k in range(4):
         at = lax.rem(h + 4 - k, 4)
-        pack_ref[at, core] = ref[0]
-        pack_ref[at, 1 - core] = ref[1]
+        pack_ref[at, core] = own_ref[k]
+        pack_ref[at, 1 - core] = other_ref[k]
     for k, ref in enumerate((g00_ref, g01_ref, g11_ref, gvv_ref)):
         unpacked(pack_ref.at[k], ref)
     g01 = g01_ref[...]
@@ -297,8 +330,8 @@
     r = jnp.where(live, r_ref[...], 0.0)
     at = pl.multiple_of(h * rows, rows)
     im = im_ref[pl.ds(at, rows), :]
-    v = im - SHIFT * w_ref[:rows, :].astype(F32)
-    av = jnp.where(live, mine_ref[...].astype(F32) - ret_ref[...].astype(F32), 0.0)
+    v = im - SHIFT * w_ref[...].astype(F32)
+    av = jnp.where(live, mine_ref[...].astype(F32) - weight(has_next()) * ret_ref[...].astype(F32), 0.0)
     sol_ref[...] = mm3(r, cr) + mm3(v, cv)
     res_ref[...] = r - mm3(im, cr) - mm3(av, cv)
 
@@ -311,43 +344,45 @@
     owned = rows * lax.axis_size("help")
     r = right_side.reshape(rows, cols)
     f = operator_panels.reshape(slots * panel, wide)
-    later = shifted(halo_map.reshape(halo), SUB, -1)
+    later = turned(halo_map.reshape(halo), SUB, -1)
     later_col, later_row = later.reshape(halo, 1), later.reshape(1, halo)
     map_col, map_row = halo_map.reshape(halo, 1), halo_map.reshape(1, halo)
 
-    (low,) = call(lower_body, (counts, panel_index, r), [((rows + 16, cols), BF)], small=2, name="lower")
-    others = from_others(low, "help")
+    row_ids = lax.axis_index("help") * rows + jnp.arange(rows, dtype=jnp.int32)
+    low = jnp.where(row_ids[:, None] < counts, r, 0.0).astype(BF)
     wg, pick = call(
         pick_body,
-        (low, *others, later_col),
-        [((owned, cols), BF), ((halo + 16, cols), BF)],
+        (low, *from_others(low, "help"), later_col),
+        [((owned, cols), BF), ((halo, cols), BF)],
         small=0,
         name="pick",
     )
-    bor = shifted(pick, SUB, 1)
-    (early,) = call(early_body, (f, wg), [((slots * panel, cols), F32)], small=0, name="early")
-    index = jnp.concatenate([panel_index, *(o[rows, :slots].astype(jnp.int32) for o in others)])
-    (z,) = call(first_body, (f, early, bor), [((slots * panel, cols), BF)], small=0, name="first")
-    zs = from_others(z, "help")
-    zg, zh, zpick = call(
+    bor = turned(pick, SUB, 1)
+    early, info = call(
+        early_body, (panel_index, f, wg), [((slots * panel, cols), F32), ((16, cols), BF)], name="early"
+    )
+    (z,) = call(
+        first_body, (f, early, info, bor), [((slots * panel + 16, cols), BF)], small=0, name="first"
+    )
+    zg, zh, zpick, index = call(
         spread_body,
-        (counts, index, z, *zs, later_col),
-        [((wide, cols), BF), ((halo, cols), BF), ((halo, cols), BF)],
+        (counts, panel_index, z, *from_others(z, "help"), later_col),
+        [((wide, cols), BF), ((halo, cols), BF), ((halo + 16, cols), BF), ((12,), jnp.int32)],
         small=2,
         name="spread",
-    )
-    ret = shifted(zh, SUB, -1)
-    zp = shifted(zpick, SUB, 1)
+        tail=scalars(),
+    )
+    ret = turned(zh, SUB, -1)
+    zp = turned(zpick, SUB, 1)
     z2, im, vb, vh = call(
         second_body,
         (counts, f, zg, ret, zp, bor, wg, map_col, later_row),
         [((slots * panel, cols), BF), ((owned, cols), F32), ((owned, cols), BF), ((halo, cols), BF)],
         name="second",
     )
-    z2s = from_others(z2, "help")
     keep, give, z2g = call(
         gram_body,
-        (index, z2, *z2s, wg, bor, zg, im, vb, vh),
+        (index, z2, *from_others(z2, "help"), wg, bor, zg, im, vb, vh),
         [((half + 8, half), F32), ((half + 8, half), F32), ((wide, cols), BF)],
         scratch=[pltpu.VMEM((cols, cols), F32), pltpu.VMEM((2, half + 8, half), F32)],
         name="gram",
@@ -356,14 +391,15 @@
     mine, back = call(
         tail_body, (z2g, map_row), [((rows, cols), BF), ((rows, cols), BF)], small=0, name="tail"
     )
-    ret2 = shifted(back, SUB, -1)
     pack = summed(pack, "sub_0")
+    pack, back = lax.optimization_barrier((pack, back))
+    ret2 = turned(back, SUB, -1)
     pack = summed(pack, "sub_1")
-    pack = jnp.stack([pack, turned(pack, "sub_2", 1)])
-    packs = from_others(pack, "help")
+    pack, ret2 = lax.optimization_barrier((pack, ret2))
+    packs = jnp.stack([pack, *from_others(pack, "help")])
     sol, res = call(
         solve_body,
-        (counts, pack, *packs, r, im, low, mine, ret2),
+        (counts, packs, turned(packs, "sub_2", 1), r, im, low, mine, ret2),
         [((rows, cols), F32), ((rows, cols), F32)],
         scratch=[pltpu.VMEM((4, 2, half + 8, half), F32)] + [pltpu.VMEM((cols, cols), F32)] * 5,
         name="solve",

time: 127 us -> 119 us (0.937)
  starting transfers between devices: 43.1 us -> 33.5 us
  waiting for transfers between devices: 44.8 us -> 47.3 us
  local copies, waits for them, and re-layouts: 1.91 us -> 0.3 us
    ppermute x5 -> x0, starting transfers between devices: 20.1 us -> none  [shifted(): return lax.ppermute(value, axis, pairs)]
    ppermute x20 -> x25, waiting for transfers between devices: 31.8 us -> 47.3 us  [turned(): lax.ppermute(value, axis, [(i, (i + by) % devices) for i in range(devices)])]
    ppermute x5 -> x0, waiting for transfers between devices: 13 us -> none  [shifted(): return lax.ppermute(value, axis, pairs)]
    ppermute x20 -> x25, starting transfers between devices: 23 us -> 33.5 us  [turned(): lax.ppermute(value, axis, [(i, (i + by) % devices) for i in range(devices)])]
    unnamed x12 -> x8, local copies, waits for them, and re-layouts: 1.62 us -> 0.02 us
    pallas_call x9 -> x8, Pallas kernels: 35.4 us -> 35.4 us  [call(): pl.pallas_call(body, in_specs=specs, out_specs=[whole() for _ in outs[1:]...]
  transfers between devices with their start and end apart: 25 -> 25, of which waited for: 20 -> 20; matrix products, arithmetic and copies ran while one was open for 0% -> 0% of each run, Pallas kernels for 0% -> 1%
where the time goes in v3:
time: 119 us
  waiting for transfers between devices  47.3 us (40%)
  Pallas kernels  35.4 us (30%)
  starting transfers between devices  33.5 us (28%)
  between operations  1.53 us (1%)
    ppermute x25, waiting for transfers between devices, turned(): lax.ppermute(value, axis, [(i, (i + by) % devices) for i in range(devices)])  47.3 us
    pallas_call x8, Pallas kernels, call(): pl.pallas_call(body, in_specs=specs, out_specs=[whole() for _ in outs[1:]...  35.4 us
    ppermute x25, starting transfers between devices, turned(): lax.ppermute(value, axis, [(i, (i + by) % devices) for i in range(devices)])  33.5 us
  transfers between devices with their start and end apart: 25, of which 20 were waited for; matrix products, arithmetic and copies ran while one was open for 0% of the time, Pallas kernels for 1%

profile of v3, /device:TPU:1, one launch (start us, length us, event | category | flops | bytes accessed | tf_op | source)
XLA Modules:
  0.0 119.1 jit_solution(6919195003571378190)
XLA Ops:
  1.4 1.1 select_convert_fusion.own_ref.w_ref
  2.5 3.6 %collective-permute-start.2 = (bf16[256,256]{1,0:T(8,128)(2,1)S(1)}, bf16[256,256]{1,0:T(8,128)(2,1)S(1)}, u32[]{:S(2)}, u32[]{:S(2)}) collective-permute-start(bf16[256,256]{1,0:T(8,128)(2,1)S(1)} %select_convert_fusion.own_ref.w_ref), channel_id=1, source_target_pairs={{0,3},{1,0},{2,1},{3,2},{4,7},{5,4},{6,5},{7,6},{8,11},{9,8},{10,9... | collective-permute-start | bytes 393224 | tf_op jit(solution)/shard_map/ppermute | solution.py:18
  6.1 0.3 collective-permute-start.1
  6.4 0.7 collective-permute-start
  7.1 1.5 %collective-permute-start.3 = (s32[512]{0:T(512)}, s32[512]{0:T(512)S(1)}, u32[]{:S(2)}, u32[]{:S(2)}) collective-permute-start(s32[512]{0:T(512)} %bitcast.21), channel_id=1, source_target_pairs={{0,124},{4,0},{8,4},{12,8},{16,12},{20,16},{24,20},{28,24},{32,28}... | collective-permute-start | bytes 6152 | tf_op jit(solution)/shard_map/ppermute | solution.py:18
  8.6 3.3 %collective-permute-done.3 = s32[512]{0:T(512)S(1)} collective-permute-done((s32[512]{0:T(512)}, s32[512]{0:T(512)S(1)}, u32[]{:S(2)}, u32[]{:S(2)}) %collective-permute-start.3) | collective-permute-done | bytes 2080 | tf_op jit(solution)/shard_map/ppermute | solution.py:18
  12.1 3.6 %collective-permute-done.a_ref = bf16[256,256]{1,0:T(8,128)(2,1)S(1)} collective-permute-done((bf16[256,256]{1,0:T(8,128)(2,1)S(1)}, bf16[256,256]{1,0:T(8,128)(2,1)S(1)}, u32[]{:S(2)}, u32[]{:S(2)}) %collective-permute-start) | collective-permute-done | bytes 131104 | tf_op jit(solution)/shard_map/ppermute | solution.py:18
  15.7 0.6 pick.1
  16.4 2.2 %collective-permute-start.4 = (bf16[512,256]{1,0:T(8,128)(2,1)S(1)}, bf16[512,256]{1,0:T(8,128)(2,1)S(1)}, u32[]{:S(2)}, u32[]{:S(2)}) collective-permute-start(bf16[512,256]{1,0:T(8,128)(2,1)S(1)} %get-tuple-element.28), channel_id=1, source_target_pairs={{0,4},{4,8},{8,12},{12,16},{16,20},{20,24},{24,28},{28,32},{32,36}... | collective-permute-start | bytes 786440 | tf_op jit(solution)/shard_map/ppermute | solution.py:18
  18.6 0.9 early.1
  19.5 2.4 %collective-permute-done.4.halo_ref.bor_ref = bf16[512,256]{1,0:T(8,128)(2,1)S(1)} collective-permute-done((bf16[512,256]{1,0:T(8,128)(2,1)S(1)}, bf16[512,256]{1,0:T(8,128)(2,1)S(1)}, u32[]{:S(2)}, u32[]{:S(2)}) %collective-permute-start.4) | collective-permute-done | bytes 262176 | tf_op jit(solution)/shard_map/ppermute | solution.py:18
  22.1 0.4 collective-permute-start.7
  22.5 0.3 collective-permute-start.6
  22.8 0.8 collective-permute-start.5
  23.7 3.1 %collective-permute-done.7.c_ref = bf16[400,256]{1,0:T(8,128)(2,1)S(1)} collective-permute-done((bf16[400,256]{1,0:T(8,128)(2,1)S(1)}, bf16[400,256]{1,0:T(8,128)(2,1)S(1)}, u32[]{:S(2)}, u32[]{:S(2)}) %collective-permute-start.7) | collective-permute-done | bytes 204832 | tf_op jit(solution)/shard_map/ppermute | solution.py:18
  26.8 1.9 %collective-permute-done.6.b_ref = bf16[400,256]{1,0:T(8,128)(2,1)S(1)} collective-permute-done((bf16[400,256]{1,0:T(8,128)(2,1)S(1)}, bf16[400,256]{1,0:T(8,128)(2,1)S(1)}, u32[]{:S(2)}, u32[]{:S(2)}) %collective-permute-start.6) | collective-permute-done | bytes 204832 | tf_op jit(solution)/shard_map/ppermute | solution.py:18
  28.7 2.1 %collective-permute-done.5.a_ref = bf16[400,256]{1,0:T(8,128)(2,1)S(1)} collective-permute-done((bf16[400,256]{1,0:T(8,128)(2,1)S(1)}, bf16[400,256]{1,0:T(8,128)(2,1)S(1)}, u32[]{:S(2)}, u32[]{:S(2)}) %collective-permute-start.5) | collective-permute-done | bytes 204832 | tf_op jit(solution)/shard_map/ppermute | solution.py:18
  30.8 1.9 %spread.1 = (bf16[1536,256]{1,0:T(8,128)(2,1)S(1)}, bf16[512,256]{1,0:T(8,128)(2,1)}, bf16[528,256]{1,0:T(8,128)(2,1)}, s32[12]{0:T(128)S(1)}) custom-call(s32[1]{0:T(128)} %copy.10.count, s32[3]{0:T(128)S(1)} %copy-done.3, bf16[400,256]{1,0:T(8,128)(2,1)S(1)} %first.1.own_ref, bf16[400,256]{1,0:T(8,128)(2,1)S(1)} %collective-permute-done.5.a_ref, ...), custom_call_target="tpu_custom_call" | custom-call | tf_op jit(solution)/shard_map/spread/pallas_call | solution.py:42
  32.7 6.7 %collective-permute-start.9 = (bf16[528,256]{1,0:T(8,128)(2,1)}, bf16[528,256]{1,0:T(8,128)(2,1)S(1)}, u32[]{:S(2)}, u32[]{:S(2)}) collective-permute-start(bf16[528,256]{1,0:T(8,128)(2,1)} %get-tuple-element.32), channel_id=1, source_target_pairs={{0,4},{4,8},{8,12},{12,16},{16,20},{20,24},{24,28},{28,32},{32,36}... | collective-permute-start | bytes 811016 | tf_op jit(solution)/shard_map/ppermute | solution.py:18
  39.5 6.1 %collective-permute-done.8.ret_ref = bf16[512,256]{1,0:T(8,128)(2,1)} collective-permute-done((bf16[512,256]{1,0:T(8,128)(2,1)}, bf16[512,256]{1,0:T(8,128)(2,1)}, u32[]{:S(2)}, u32[]{:S(2)}) %collective-permute-start.8) | collective-permute-done | bytes 262176 | tf_op jit(solution)/shard_map/ppermute | solution.py:18
  45.7 2.2 %second.1 = (bf16[384,256]{1,0:T(8,128)(2,1)S(1)}, f32[1024,256]{1,0:T(8,128)S(1)}, bf16[1024,256]{1,0:T(8,128)(2,1)S(1)}, bf16[512,256]{1,0:T(8,128)(2,1)S(1)}) custom-call(s32[1]{0:T(128)} %copy.10.count, bf16[384,1536]{1,0:T(8,128)(2,1)S(1)} %bitcast.17, bf16[1536,256]{1,0:T(8,128)(2,1)S(1)} %get-tuple-element.30.zg_ref, ...), custom_call_target="tpu_custom_call" | custom-call | tf_op jit(solution)/shard_map/second/pallas_call | solution.py:42
  47.9 0.7 collective-permute-start.12
  48.6 0.9 collective-permute-start.10
  49.5 3.1 %collective-permute-done.12.c_ref = bf16[384,256]{1,0:T(8,128)(2,1)S(1)} collective-permute-done((bf16[384,256]{1,0:T(8,128)(2,1)S(1)}, bf16[384,256]{1,0:T(8,128)(2,1)S(1)}, u32[]{:S(2)}, u32[]{:S(2)}) %collective-permute-start.12) | collective-permute-done | bytes 196640 | tf_op jit(solution)/shard_map/ppermute | solution.py:18
  52.5 2.2 %collective-permute-done.11.b_ref = bf16[384,256]{1,0:T(8,128)(2,1)S(1)} collective-permute-done((bf16[384,256]{1,0:T(8,128)(2,1)S(1)}, bf16[384,256]{1,0:T(8,128)(2,1)S(1)}, u32[]{:S(2)}, u32[]{:S(2)}) %collective-permute-start.11) | collective-permute-done | bytes 196640 | tf_op jit(solution)/shard_map/ppermute | solution.py:18
  54.7 4.6 %collective-permute-done.10.a_ref = bf16[384,256]{1,0:T(8,128)(2,1)S(1)} collective-permute-done((bf16[384,256]{1,0:T(8,128)(2,1)S(1)}, bf16[384,256]{1,0:T(8,128)(2,1)S(1)}, u32[]{:S(2)}, u32[]{:S(2)}) %collective-permute-start.10) | collective-permute-done | bytes 196640 | tf_op jit(solution)/shard_map/ppermute | solution.py:18
  59.3 1.1 gram.1
  60.4 2.4 %collective-permute-start.13 = (f32[136,128]{1,0:T(8,128)S(1)}, f32[136,128]{1,0:T(8,128)S(1)}, u32[]{:S(2)}, u32[]{:S(2)}) collective-permute-start(f32[136,128]{1,0:T(8,128)S(1)} %get-tuple-element.38), channel_id=1, source_target_pairs={{0,4},{4,0},{1,5},{5,1},{2,6},{6,2},{3,7},{7,3},{8,12},{12,8},{9,1... | collective-permute-start | bytes 208904 | tf_op jit(solution)/shard_map/ppermute | solution.py:18
  62.8 0.9 collective-permute-done.13
  63.7 2.5 %collective-permute-start.16 = (f32[136,128]{1,0:T(8,128)S(1)}, f32[136,128]{1,0:T(8,128)S(1)}, u32[]{:S(2)}, u32[]{:S(2)}) collective-permute-start(f32[136,128]{1,0:T(8,128)S(1)} %add.33), channel_id=1, source_target_pairs={{0,96},{32,0},{64,32},{96,64},{1,97},{33,1},{65,33},{97,65},{2,98}... | collective-permute-start | bytes 208904 | tf_op jit(solution)/shard_map/ppermute | solution.py:18
  66.2 0.5 collective-permute-start.15
  66.8 0.6 collective-permute-start.14
  67.6 3.3 %collective-permute-done.15 = f32[136,128]{1,0:T(8,128)S(1)} collective-permute-done((f32[136,128]{1,0:T(8,128)S(1)}, f32[136,128]{1,0:T(8,128)S(1)}, u32[]{:S(2)}, u32[]{:S(2)}) %collective-permute-start.15) | collective-permute-done | bytes 69664 | tf_op jit(solution)/shard_map/ppermute | solution.py:18
  71.0 1.9 %collective-permute-done.14 = f32[136,128]{1,0:T(8,128)S(1)} collective-permute-done((f32[136,128]{1,0:T(8,128)S(1)}, f32[136,128]{1,0:T(8,128)S(1)}, u32[]{:S(2)}, u32[]{:S(2)}) %collective-permute-start.14) | collective-permute-done | bytes 69664 | tf_op jit(solution)/shard_map/ppermute | solution.py:18
  72.9 0.9 collective-permute-start.19
  73.7 1.6 %collective-permute-start.18 = (f32[136,128]{1,0:T(8,128)S(1)}, f32[136,128]{1,0:T(8,128)S(1)}, u32[]{:S(2)}, u32[]{:S(2)}) collective-permute-start(f32[136,128]{1,0:T(8,128)S(1)} %add_add_fusion.1), channel_id=1, source_target_pairs={{0,16},{8,24},{16,0},{24,8},{1,17},{9,25},{17,1},{25,9},{2,18},{10... | collective-permute-start | bytes 208904 | tf_op jit(solution)/shard_map/ppermute | solution.py:18
  75.3 1.6 %collective-permute-start.20 = (bf16[256,256]{1,0:T(8,128)(2,1)S(1)}, bf16[256,256]{1,0:T(8,128)(2,1)S(1)}, u32[]{:S(2)}, u32[]{:S(2)}) collective-permute-start(bf16[256,256]{1,0:T(8,128)(2,1)S(1)} %get-tuple-element.42), channel_id=1, source_target_pairs={{0,124},{4,0},{8,4},{12,8},{16,12},{20,16},{24,20},{28,24},{32,28}... | collective-permute-start | bytes 393224 | tf_op jit(solution)/shard_map/ppermute | solution.py:18
  76.9 1.5 %collective-permute-done.18 = f32[136,128]{1,0:T(8,128)S(1)} collective-permute-done((f32[136,128]{1,0:T(8,128)S(1)}, f32[136,128]{1,0:T(8,128)S(1)}, u32[]{:S(2)}, u32[]{:S(2)}) %collective-permute-start.18) | collective-permute-done | bytes 69664 | tf_op jit(solution)/shard_map/ppermute | solution.py:18
  78.4 2.1 %collective-permute-done.17 = f32[136,128]{1,0:T(8,128)S(1)} collective-permute-done((f32[136,128]{1,0:T(8,128)S(1)}, f32[136,128]{1,0:T(8,128)S(1)}, u32[]{:S(2)}, u32[]{:S(2)}) %collective-permute-start.17) | collective-permute-done | bytes 69664 | tf_op jit(solution)/shard_map/ppermute | solution.py:18
  80.7 0.4 collective-permute-start.23
  81.1 1.1 collective-permute-start.22
  82.3 0.6 collective-permute-start.21
  82.9 1.0 collective-permute-done.23
  83.9 1.9 %collective-permute-done.22 = f32[136,128]{1,0:T(8,128)S(1)} collective-permute-done((f32[136,128]{1,0:T(8,128)S(1)}, f32[136,128]{1,0:T(8,128)S(1)}, u32[]{:S(2)}, u32[]{:S(2)}) %collective-permute-start.22) | collective-permute-done | bytes 69664 | tf_op jit(solution)/shard_map/ppermute | solution.py:18
  85.8 0.8 collective-permute-done.21
  86.6 3.1 %collective-permute-start.24 = (f32[4,136,128]{2,1,0:T(8,128)S(1)}, f32[4,136,128]{2,1,0:T(8,128)S(1)}, u32[]{:S(2)}, u32[]{:S(2)}) collective-permute-start(f32[4,136,128]{2,1,0:T(8,128)S(1)} %pad_maximum_fusion.own_ref), channel_id=1, source_target_pairs={{0,4},{4,0},{1,5},{5,1},{2,6},{6,2},{3,7},{7,3},{8,12},{12,8},{9,1... | collective-permute-start | bytes 835592 | tf_op jit(solution)/shard_map/ppermute | solution.py:18
  89.8 1.2 collective-permute-done.24.other_ref
  91.0 28.1 %solve.1 = (f32[256,256]{1,0:T(8,128)}, f32[256,256]{1,0:T(8,128)}) custom-call(s32[1]{0:T(128)} %copy.10.count, f32[4,136,128]{2,1,0:T(8,128)S(1)} %pad_maximum_fusion.own_ref, f32[4,136,128]{2,1,0:T(8,128)S(1)} %collective-permute-done.24.other_ref, f32[256,256]{1,0:T(8,128)S(1)} %bitcast.18, f32[1024,256]{1,0:T(8,128)S(1)} %get-tuple-element.34.im_ref, ...), custom_call_target="tpu_custom_call" | custom-call | tf_op jit(solution)/shard_map/solve/pallas_call | solution.py:42
  (26 shorter events, 1.1 us)
Async XLA Ops:
  0.6 17.9 %copy-start.3 = (s32[3]{0:T(128)S(1)}, s32[3]{0:T(128)}, u32[]{:S(2)}) copy-start(s32[3]{0:T(128)} %index.3) | copy-start | bytes 40
  0.6 17.9 %copy-start = (bf16[3,128,1536]{2,1,0:T(8,128)(2,1)S(1)}, bf16[3,128,1536]{2,1,0:T(8,128)(2,1)}, u32[]{:S(2)}) copy-start(bf16[3,128,1536]{2,1,0:T(8,128)(2,1)} %param.6) | copy-start | bytes 3538948
  2.5 9.6 %collective-permute-start.2 = (bf16[256,256]{1,0:T(8,128)(2,1)S(1)}, bf16[256,256]{1,0:T(8,128)(2,1)S(1)}, u32[]{:S(2)}, u32[]{:S(2)}) collective-permute-start(bf16[256,256]{1,0:T(8,128)(2,1)S(1)} %select_convert_fusion.own_ref.w_ref), channel_id=1, source_target_pairs={{0,3},{1,0},{2,1},{3,2},{4,7},{5,4},{6,5},{7,6},{8,11},{9,8},{10,9... | collective-permute-start | bytes 393224 | tf_op jit(solution)/shard_map/ppermute | solution.py:18
  6.1 6.0 %collective-permute-start.1 = (bf16[256,256]{1,0:T(8,128)(2,1)S(1)}, bf16[256,256]{1,0:T(8,128)(2,1)S(1)}, u32[]{:S(2)}, u32[]{:S(2)}) collective-permute-start(bf16[256,256]{1,0:T(8,128)(2,1)S(1)} %select_convert_fusion.own_ref.w_ref), channel_id=1, source_target_pairs={{0,2},{1,3},{2,0},{3,1},{4,6},{5,7},{6,4},{7,5},{8,10},{9,11},{10,... | collective-permute-start | bytes 393224 | tf_op jit(solution)/shard_map/ppermute | solution.py:18
  6.4 9.3 %collective-permute-start = (bf16[256,256]{1,0:T(8,128)(2,1)S(1)}, bf16[256,256]{1,0:T(8,128)(2,1)S(1)}, u32[]{:S(2)}, u32[]{:S(2)}) collective-permute-start(bf16[256,256]{1,0:T(8,128)(2,1)S(1)} %select_convert_fusion.own_ref.w_ref), channel_id=1, source_target_pairs={{0,1},{1,2},{2,3},{3,0},{4,5},{5,6},{6,7},{7,4},{8,9},{9,10},{10,1... | collective-permute-start | bytes 393224 | tf_op jit(solution)/shard_map/ppermute | solution.py:18
  7.1 4.8 %collective-permute-start.3 = (s32[512]{0:T(512)}, s32[512]{0:T(512)S(1)}, u32[]{:S(2)}, u32[]{:S(2)}) collective-permute-start(s32[512]{0:T(512)} %bitcast.21), channel_id=1, source_target_pairs={{0,124},{4,0},{8,4},{12,8},{16,12},{20,16},{24,20},{28,24},{32,28}... | collective-permute-start | bytes 6152 | tf_op jit(solution)/shard_map/ppermute | solution.py:18
  16.4 5.5 %collective-permute-start.4 = (bf16[512,256]{1,0:T(8,128)(2,1)S(1)}, bf16[512,256]{1,0:T(8,128)(2,1)S(1)}, u32[]{:S(2)}, u32[]{:S(2)}) collective-permute-start(bf16[512,256]{1,0:T(8,128)(2,1)S(1)} %get-tuple-element.28), channel_id=1, source_target_pairs={{0,4},{4,8},{8,12},{12,16},{16,20},{20,24},{24,28},{28,32},{32,36}... | collective-permute-start | bytes 786440 | tf_op jit(solution)/shard_map/ppermute | solution.py:18
  21.9 17.5 %copy-start.2 = (s32[1,512]{1,0:T(1,128)S(1)}, s32[1,512]{1,0:T(1,128)}, u32[]{:S(2)}) copy-start(s32[1,512]{1,0:T(1,128)} %map_ref.1) | copy-start | bytes 6148
  22.1 4.7 %collective-permute-start.7 = (bf16[400,256]{1,0:T(8,128)(2,1)S(1)}, bf16[400,256]{1,0:T(8,128)(2,1)S(1)}, u32[]{:S(2)}, u32[]{:S(2)}) collective-permute-start(bf16[400,256]{1,0:T(8,128)(2,1)S(1)} %first.1.own_ref), channel_id=1, source_target_pairs={{0,3},{1,0},{2,1},{3,2},{4,7},{5,4},{6,5},{7,6},{8,11},{9,8},{10,9... | collective-permute-start | bytes 614408 | tf_op jit(solution)/shard_map/ppermute | solution.py:18
  22.5 6.2 %collective-permute-start.6 = (bf16[400,256]{1,0:T(8,128)(2,1)S(1)}, bf16[400,256]{1,0:T(8,128)(2,1)S(1)}, u32[]{:S(2)}, u32[]{:S(2)}) collective-permute-start(bf16[400,256]{1,0:T(8,128)(2,1)S(1)} %first.1.own_ref), channel_id=1, source_target_pairs={{0,2},{1,3},{2,0},{3,1},{4,6},{5,7},{6,4},{7,5},{8,10},{9,11},{10,... | collective-permute-start | bytes 614408 | tf_op jit(solution)/shard_map/ppermute | solution.py:18
  22.8 8.0 %collective-permute-start.5 = (bf16[400,256]{1,0:T(8,128)(2,1)S(1)}, bf16[400,256]{1,0:T(8,128)(2,1)S(1)}, u32[]{:S(2)}, u32[]{:S(2)}) collective-permute-start(bf16[400,256]{1,0:T(8,128)(2,1)S(1)} %first.1.own_ref), channel_id=1, source_target_pairs={{0,1},{1,2},{2,3},{3,0},{4,5},{5,6},{6,7},{7,4},{8,9},{9,10},{10,1... | collective-permute-start | bytes 614408 | tf_op jit(solution)/shard_map/ppermute | solution.py:18
  32.7 13.0 %collective-permute-start.9 = (bf16[528,256]{1,0:T(8,128)(2,1)}, bf16[528,256]{1,0:T(8,128)(2,1)S(1)}, u32[]{:S(2)}, u32[]{:S(2)}) collective-permute-start(bf16[528,256]{1,0:T(8,128)(2,1)} %get-tuple-element.32), channel_id=1, source_target_pairs={{0,4},{4,8},{8,12},{12,16},{16,20},{20,24},{24,28},{28,32},{32,36}... | collective-permute-start | bytes 811016 | tf_op jit(solution)/shard_map/ppermute | solution.py:18
  39.4 6.3 %collective-permute-start.8 = (bf16[512,256]{1,0:T(8,128)(2,1)}, bf16[512,256]{1,0:T(8,128)(2,1)}, u32[]{:S(2)}, u32[]{:S(2)}) collective-permute-start(bf16[512,256]{1,0:T(8,128)(2,1)} %get-tuple-element.31), channel_id=1, source_target_pairs={{0,124},{4,0},{8,4},{12,8},{16,12},{20,16},{24,20},{28,24},{32,28}... | collective-permute-start | bytes 786440 | tf_op jit(solution)/shard_map/ppermute | solution.py:18
  47.9 4.6 %collective-permute-start.12 = (bf16[384,256]{1,0:T(8,128)(2,1)S(1)}, bf16[384,256]{1,0:T(8,128)(2,1)S(1)}, u32[]{:S(2)}, u32[]{:S(2)}) collective-permute-start(bf16[384,256]{1,0:T(8,128)(2,1)S(1)} %get-tuple-element.33.own_ref), channel_id=1, source_target_pairs={{0,3},{1,0},{2,1},{3,2},{4,7},{5,4},{6,5},{7,6},{8,11},{9,8},{10,9... | collective-permute-start | bytes 589832 | tf_op jit(solution)/shard_map/ppermute | solution.py:18
  48.6 6.1 %collective-permute-start.11 = (bf16[384,256]{1,0:T(8,128)(2,1)S(1)}, bf16[384,256]{1,0:T(8,128)(2,1)S(1)}, u32[]{:S(2)}, u32[]{:S(2)}) collective-permute-start(bf16[384,256]{1,0:T(8,128)(2,1)S(1)} %get-tuple-element.33.own_ref), channel_id=1, source_target_pairs={{0,2},{1,3},{2,0},{3,1},{4,6},{5,7},{6,4},{7,5},{8,10},{9,11},{10,... | collective-permute-start | bytes 589832 | tf_op jit(solution)/shard_map/ppermute | solution.py:18
  48.6 10.7 %collective-permute-start.10 = (bf16[384,256]{1,0:T(8,128)(2,1)S(1)}, bf16[384,256]{1,0:T(8,128)(2,1)S(1)}, u32[]{:S(2)}, u32[]{:S(2)}) collective-permute-start(bf16[384,256]{1,0:T(8,128)(2,1)S(1)} %get-tuple-element.33.own_ref), channel_id=1, source_target_pairs={{0,1},{1,2},{2,3},{3,0},{4,5},{5,6},{6,7},{7,4},{8,9},{9,10},{10,1... | collective-permute-start | bytes 589832 | tf_op jit(solution)/shard_map/ppermute | solution.py:18
  60.4 30.6 %copy-start.1 = (f32[1,256,256]{2,1,0:T(8,128)S(1)}, f32[1,256,256]{2,1,0:T(8,128)}, u32[]{:S(2)}) copy-start(f32[1,256,256]{2,1,0:T(8,128)} %param.5) | copy-start | bytes 786436
  60.4 3.3 %collective-permute-start.13 = (f32[136,128]{1,0:T(8,128)S(1)}, f32[136,128]{1,0:T(8,128)S(1)}, u32[]{:S(2)}, u32[]{:S(2)}) collective-permute-start(f32[136,128]{1,0:T(8,128)S(1)} %get-tuple-element.38), channel_id=1, source_target_pairs={{0,4},{4,0},{1,5},{5,1},{2,6},{6,2},{3,7},{7,3},{8,12},{12,8},{9,1... | collective-permute-start | bytes 208904 | tf_op jit(solution)/shard_map/ppermute | solution.py:18
  63.7 3.9 %collective-permute-start.16 = (f32[136,128]{1,0:T(8,128)S(1)}, f32[136,128]{1,0:T(8,128)S(1)}, u32[]{:S(2)}, u32[]{:S(2)}) collective-permute-start(f32[136,128]{1,0:T(8,128)S(1)} %add.33), channel_id=1, source_target_pairs={{0,96},{32,0},{64,32},{96,64},{1,97},{33,1},{65,33},{97,65},{2,98}... | collective-permute-start | bytes 208904 | tf_op jit(solution)/shard_map/ppermute | solution.py:18
  66.2 4.7 %collective-permute-start.15 = (f32[136,128]{1,0:T(8,128)S(1)}, f32[136,128]{1,0:T(8,128)S(1)}, u32[]{:S(2)}, u32[]{:S(2)}) collective-permute-start(f32[136,128]{1,0:T(8,128)S(1)} %add.33), channel_id=1, source_target_pairs={{0,64},{32,96},{64,0},{96,32},{1,65},{33,97},{65,1},{97,33},{2,66}... | collective-permute-start | bytes 208904 | tf_op jit(solution)/shard_map/ppermute | solution.py:18
  66.8 6.1 %collective-permute-start.14 = (f32[136,128]{1,0:T(8,128)S(1)}, f32[136,128]{1,0:T(8,128)S(1)}, u32[]{:S(2)}, u32[]{:S(2)}) collective-permute-start(f32[136,128]{1,0:T(8,128)S(1)} %add.33), channel_id=1, source_target_pairs={{0,32},{32,64},{64,96},{96,0},{1,33},{33,65},{65,97},{97,1},{2,34}... | collective-permute-start | bytes 208904 | tf_op jit(solution)/shard_map/ppermute | solution.py:18
  72.9 4.0 %collective-permute-start.19 = (f32[136,128]{1,0:T(8,128)S(1)}, f32[136,128]{1,0:T(8,128)S(1)}, u32[]{:S(2)}, u32[]{:S(2)}) collective-permute-start(f32[136,128]{1,0:T(8,128)S(1)} %add_add_fusion.1), channel_id=1, source_target_pairs={{0,24},{8,0},{16,8},{24,16},{1,25},{9,1},{17,9},{25,17},{2,26},{10... | collective-permute-start | bytes 208904 | tf_op jit(solution)/shard_map/ppermute | solution.py:18
  73.7 4.7 %collective-permute-start.18 = (f32[136,128]{1,0:T(8,128)S(1)}, f32[136,128]{1,0:T(8,128)S(1)}, u32[]{:S(2)}, u32[]{:S(2)}) collective-permute-start(f32[136,128]{1,0:T(8,128)S(1)} %add_add_fusion.1), channel_id=1, source_target_pairs={{0,16},{8,24},{16,0},{24,8},{1,17},{9,25},{17,1},{25,9},{2,18},{10... | collective-permute-start | bytes 208904 | tf_op jit(solution)/shard_map/ppermute | solution.py:18
  75.3 5.1 %collective-permute-start.17 = (f32[136,128]{1,0:T(8,128)S(1)}, f32[136,128]{1,0:T(8,128)S(1)}, u32[]{:S(2)}, u32[]{:S(2)}) collective-permute-start(f32[136,128]{1,0:T(8,128)S(1)} %add_add_fusion.1), channel_id=1, source_target_pairs={{0,8},{8,16},{16,24},{24,0},{1,9},{9,17},{17,25},{25,1},{2,10},{10... | collective-permute-start | bytes 208904 | tf_op jit(solution)/shard_map/ppermute | solution.py:18
  75.3 5.4 %collective-permute-start.20 = (bf16[256,256]{1,0:T(8,128)(2,1)S(1)}, bf16[256,256]{1,0:T(8,128)(2,1)S(1)}, u32[]{:S(2)}, u32[]{:S(2)}) collective-permute-start(bf16[256,256]{1,0:T(8,128)(2,1)S(1)} %get-tuple-element.42), channel_id=1, source_target_pairs={{0,124},{4,0},{8,4},{12,8},{16,12},{20,16},{24,20},{28,24},{32,28}... | collective-permute-start | bytes 393224 | tf_op jit(solution)/shard_map/ppermute | solution.py:18
  80.7 3.2 %collective-permute-start.23 = (f32[136,128]{1,0:T(8,128)S(1)}, f32[136,128]{1,0:T(8,128)S(1)}, u32[]{:S(2)}, u32[]{:S(2)}) collective-permute-start(f32[136,128]{1,0:T(8,128)S(1)} %add_add_fusion), channel_id=1, source_target_pairs={{0,3},{1,0},{2,1},{3,2},{4,7},{5,4},{6,5},{7,6},{8,11},{9,8},{10,9... | collective-permute-start | bytes 208904 | tf_op jit(solution)/shard_map/ppermute | solution.py:18
  81.1 4.7 %collective-permute-start.22 = (f32[136,128]{1,0:T(8,128)S(1)}, f32[136,128]{1,0:T(8,128)S(1)}, u32[]{:S(2)}, u32[]{:S(2)}) collective-permute-start(f32[136,128]{1,0:T(8,128)S(1)} %add_add_fusion), channel_id=1, source_target_pairs={{0,2},{1,3},{2,0},{3,1},{4,6},{5,7},{6,4},{7,5},{8,10},{9,11},{10,... | collective-permute-start | bytes 208904 | tf_op jit(solution)/shard_map/ppermute | solution.py:18
  82.3 4.4 %collective-permute-start.21 = (f32[136,128]{1,0:T(8,128)S(1)}, f32[136,128]{1,0:T(8,128)S(1)}, u32[]{:S(2)}, u32[]{:S(2)}) collective-permute-start(f32[136,128]{1,0:T(8,128)S(1)} %add_add_fusion), channel_id=1, source_target_pairs={{0,1},{1,2},{2,3},{3,0},{4,5},{5,6},{6,7},{7,4},{8,9},{9,10},{10,1... | collective-permute-start | bytes 208904 | tf_op jit(solution)/shard_map/ppermute | solution.py:18
  86.6 4.3 %collective-permute-start.24 = (f32[4,136,128]{2,1,0:T(8,128)S(1)}, f32[4,136,128]{2,1,0:T(8,128)S(1)}, u32[]{:S(2)}, u32[]{:S(2)}) collective-permute-start(f32[4,136,128]{2,1,0:T(8,128)S(1)} %pad_maximum_fusion.own_ref), channel_id=1, source_target_pairs={{0,4},{4,0},{1,5},{5,1},{2,6},{6,2},{3,7},{7,3},{8,12},{12,8},{9,1... | collective-permute-start | bytes 835592 | tf_op jit(solution)/shard_map/ppermute | solution.py:18
